TPU v7x, 32 devices: a whole 2x2x4 slice. The times are simulated.
32 devices in a mesh: groups: 2 (over y), gz: 4 (over z), dev: 2 (over x), xy: 2 (over core).
Axes of the slice: x: 2, y: 2, z: 4, core: 2. Of those that a mesh axis runs over, the one named last changes fastest.
Arguments:
- fields: float32 [12, 8, 64, 256], P('groups', 'dev', 'gz', 'xy'), parts along dimension 0, may hold values from -6 to 6
- spectra: float32 [24, 8, 64, 256], P('groups', 'dev', 'gz', 'xy'), parts along dimension 0, may hold values from -6 to 6
- permittivity: float32 [16, 64, 256], P(('groups', 'dev'), 'gz', 'xy'), parts along dimension 0, may hold values from 1 to 12
- phase_start: float32 [2], P('groups'), parts along dimension 0, may hold values from -3.140625 to 3.140625
- wall_owner: int32 [4, 4], P('gz'), may hold values from 0 to 3, as said below
- cap_owner: int32 [2, 32], replicated, may hold values from 0 to 3, as said below
- dir_index: int32 [2048], replicated, may hold values from 0 to 4095
- target: float32 [4096], P('groups'), parts along dimension 0, may hold values from 1 to 12
- aim_mask: int32 [4096], P('groups'), parts along dimension 0, may hold values 0 or 1
Outputs:
- fields_out: float32 [12, 8, 64, 256], P('groups', 'dev', 'gz', 'xy'), parts along dimension 0
- spectra_out: float32 [24, 8, 64, 256], P('groups', 'dev', 'gz', 'xy'), parts along dimension 0
- owned_currents: float32 [8, 2, 2, 20, 128], P(('groups', 'gz'), 'dev', 'xy'), parts along dimension 0
- intensity: float32 [4096], P(('groups', 'gz', 'dev', 'xy')), parts along dimension 0
- adjoint_currents: float32 [8, 2, 2, 36, 128], P(('groups', 'gz'), 'dev', 'xy'), parts along dimension 0
There are 2 independent parts, one for each index of `groups`. A program takes and returns all parts, laid end to end along the dimension named above; an argument that names none is the same for every part. Nothing has to cross between parts.
Inputs may be any that keep to these rules, and one draw needn't show every extreme that they name: `wall_owner`: entry [s, j] names the index of gz that owns wall patch j of slab s; every index owns exactly 4 wall patches of a column, and a slab gives one index at most 1 of them. `cap_owner`: row 0 names the owner on gz of each patch of the lower cap, row 1 of the upper cap; each index owns exactly 8 patches of each cap, so that every index owns exactly 20 patches of a column.
All inputs are finite; a program needn't handle non-finite values.
Results may differ from a plain program's by a relative error of at most 0.0003.
Values sent between devices are 32-bit elements; how exact they have to be, the bound alone decides.
A program may use at most 64 MiB of HBM per device.

v0:
```python
import functools
import math

import jax
import jax.numpy as jnp
from jax import lax
from jax.experimental import pallas as pl
from jax.experimental.pallas import tpu as pltpu
from jax.sharding import PartitionSpec as P

PATCH = 16
XB = 8
ZB = 4
STEPS = 3
THETAS = 64
COURANT = 0.5
ANGULAR_STEP = 0.3
WAVE_NUMBER = 0.6
LANES = 128
HIGHEST = lax.Precision.HIGHEST
CURRENT_SIGNS = (-1.0, 1.0, 1.0, -1.0)
X_PICKS = (5, 4, 2, 1)
Z_PICKS = (4, 3, 1, 0)
MESH = pl.DeviceIdType.MESH
AXES = ("dev", "gz", "xy")
F32 = jnp.float32
BF16 = jnp.bfloat16


def iota(shape, dim):
    return lax.broadcasted_iota(jnp.int32, shape, dim)


def sincos(turns):
    half = (turns - jnp.floor(turns + 0.5)) * math.pi
    sq = half * half
    sin_h = half * (1.0 + sq * (-1.0 / 6 + sq * (1.0 / 120 + sq * (-1.0 / 5040 + sq * (1.0 / 362880 - sq * (1.0 / 39916800))))))
    cos_h = 1.0 + sq * (-0.5 + sq * (1.0 / 24 + sq * (-1.0 / 720 + sq * (1.0 / 40320 + sq * (-1.0 / 3628800 + sq * (1.0 / 479001600))))))
    return 2.0 * sin_h * cos_h, 1.0 - 2.0 * sin_h * sin_h


def split(values):
    high = values.astype(BF16)
    return high, (values - high.astype(F32)).astype(BF16)


def block_transpose(tile):
    on_diagonal = (iota(tile.shape, 1) // PATCH) == iota(tile.shape, 0)
    total = jnp.where(on_diagonal, tile, 0.0)
    for k in range(1, 8):
        turned = pltpu.roll(tile, PATCH * k, 1)
        total = total + pltpu.roll(jnp.where(on_diagonal, turned, 0.0), 8 - k, 0)
    return total


def kernel(
    sizes,
    fields_in, spectra_in, permit_in, phase, wall_owner, cap_owner, dirs, target, aim,
    fields_out, spectra_out, owned_out, intensity_out, adjoint_out,
    send_y, send_z, send_x, got_y, got_z, got_x,
    fields, spectra, permit, geo, weights, phases, table_hi, table_lo, cap_plane, lhs,
    parts_out, parts_in, slopes, walls, caps,
    halo_send, halo_got, part_send, part_got, slope_send, slope_got, wall_send, wall_got, cap_send, cap_got, loads,
):
    slabs, devs, xys = sizes
    peers = slabs * devs * xys
    size_y, size_z, size_x = permit.shape
    chunks = dirs.shape[0]
    ratio = peers // chunks
    groups = 2 * size_y
    half_rows = 8 * size_y
    all_rows = 2 * half_rows
    gz, dev, xy = lax.axis_index("gz"), lax.axis_index("dev"), lax.axis_index("xy")
    me = (gz * devs + dev) * xys + xy
    place = {"dev": dev, "gz": gz, "xy": xy}
    count = {"dev": devs, "gz": slabs, "xy": xys}

    loading = [
        pltpu.make_async_copy(source, held, loads.at[number])
        for number, (source, held) in enumerate(((fields_in, fields), (permit_in, permit), (spectra_in, spectra)))
    ]
    for copy in loading:
        copy.start()

    def ident(flat):
        return {"gz": flat // (devs * xys), "dev": (flat // xys) % devs, "xy": flat % xys}

    barrier = pltpu.get_barrier_semaphore()

    def greet(k, carry):
        pl.semaphore_signal(barrier, inc=1, device_id=ident((me + k) % peers), device_id_type=MESH)
        return carry

    lax.fori_loop(1, peers, greet, 0)

    index = dirs[...]
    sin_t, cos_t = sincos(((index // THETAS).astype(F32) + 0.5) * (0.5 / THETAS))
    sin_f, cos_f = sincos((index % THETAS).astype(F32) * (1.0 / THETAS))
    wave = WAVE_NUMBER / (2.0 * math.pi)
    for slot, values in enumerate((
        wave * sin_t * cos_f, wave * sin_t * sin_f, wave * cos_t,
        cos_t * cos_f, cos_t * sin_f, -sin_t, -sin_f, cos_f,
    )):
        geo[slot] = values

    grid_x, grid_y, grid_z = size_x * xys, size_y * devs, size_z * slabs
    x_first = (xy * size_x).astype(F32) - (grid_x - 1) / 2.0
    y_first = (dev * size_y).astype(F32) - (grid_y - 1) / 2.0
    z_first = (gz * size_z).astype(F32) - (grid_z - 1) / 2.0
    x_wall = jnp.where(xy == 0, XB, size_x - 1 - XB)
    z_cap = jnp.where(gz == 0, ZB, size_z - 1 - ZB)
    x_face = x_first + x_wall.astype(F32)
    z_face = z_first + z_cap.astype(F32)
    facing_x = jnp.where(xy == 0, -1.0, 1.0)
    facing_z = jnp.where(gz == 0, -1.0, 1.0)
    is_end = jnp.logical_or(gz == 0, gz == slabs - 1)
    end_weight = jnp.where(is_end, 1.0, 0.0)
    norm = 1.0 / math.sqrt(2.0 * (2 * grid_y * grid_z + 2 * grid_y * grid_x))

    def make_tables(j, carry):
        def row(slot):
            return geo[slot, pl.ds(j, 1), :]

        ux, uy, uz = row(0), row(1), row(2)
        blocks = size_x // 8
        far_s, far_c = sincos((iota((blocks, LANES), 0).astype(F32) * 8.0 + x_first) * ux)
        near_s, near_c = sincos(iota((8, LANES), 0).astype(F32) * ux)
        far_s, far_c = far_s[:, None, :], far_c[:, None, :]
        near_s, near_c = near_s[None], near_c[None]
        cos_x = (far_c * near_c - far_s * near_s).reshape(size_x, LANES)
        sin_x = (far_s * near_c + far_c * near_s).reshape(size_x, LANES)
        sin_z, cos_z = sincos((iota((size_z, LANES), 0).astype(F32) + z_first) * uz)
        for at, (x_part, z_part) in enumerate(((cos_x, cos_z), (sin_x, sin_z))):
            lanes = pl.ds(at * LANES, LANES)
            x_high, x_low = split(x_part)
            z_high, z_low = split(z_part)
            table_hi[j, pl.ds(0, size_x), lanes] = x_high
            table_lo[j, pl.ds(0, size_x), lanes] = x_low
            table_hi[j, pl.ds(size_x, 8 * size_z), lanes] = jnp.concatenate([z_high] * 8, axis=0)
            table_lo[j, pl.ds(size_x, 8 * size_z), lanes] = jnp.concatenate([z_low] * 8, axis=0)
        which = iota((groups, LANES), 0)
        cell_y = (which % size_y).astype(F32) + y_first
        sin_g, cos_g = sincos(cell_y * uy + jnp.where(which < size_y, z_face * uz, x_face * ux))
        phases[j, 0] = cos_g
        phases[j, 1] = sin_g
        kind = iota((8, LANES), 0) % 4

        def pattern(a, b, c, d):
            return jnp.where(kind == 0, a, jnp.where(kind == 1, b, jnp.where(kind == 2, c, d)))

        tx, ty, tz, fx, fy = row(3), row(4), row(5), row(6), row(7)
        weights[j, 0] = pattern(-tx, -ty, -fx, -fy)
        weights[j, 1] = pattern(-fx, -fy, tx, ty)
        weights[j, 2] = pattern(-ty, -tz, -fy, jnp.zeros_like(fy))
        weights[j, 3] = pattern(-fy, jnp.zeros_like(fy), ty, tz)
        return carry

    windows = 2 * STEPS

    def tables_of(window):
        lax.fori_loop(window * chunks // windows, (window + 1) * chunks // windows, make_tables, 0)

    order = iota((8, LANES), 0).astype(F32)
    run_s, run_c = sincos((phase[...] + 0.5 * ANGULAR_STEP * (order + 1.0)) * (0.5 / math.pi))

    for number, (axis, got) in enumerate(zip(AXES, (got_y, got_z, got_x))):
        @pl.when(place[axis] == count[axis] - 1)
        def _():
            for window in range(0, windows, 2):
                got[window] = jnp.zeros(got.shape[1:], F32)

        @pl.when(place[axis] == 0)
        def _():
            for window in range(1, windows, 2):
                got[window] = jnp.zeros(got.shape[1:], F32)

    loading[0].wait()
    pl.semaphore_wait(barrier, peers - 1)

    lane = iota((size_z, LANES), 1)
    lane3 = iota((size_y, size_z, LANES), 2)
    row3 = iota((size_y, size_z, LANES), 1)

    def halo_copies(window):
        step = -1 if window % 2 == 0 else 1
        copies = []
        for number, (axis, source, landing) in enumerate(
            zip(AXES, (send_y, send_z, send_x), (got_y, got_z, got_x))
        ):
            mine, total = place[axis], count[axis]
            copy = pltpu.make_async_remote_copy(
                src_ref=source.at[window],
                dst_ref=landing.at[window],
                send_sem=halo_send.at[window, number],
                recv_sem=halo_got.at[window, number],
                device_id={axis: (mine + step + total) % total},
                device_id_type=MESH,
            )
            if step < 0:
                copies.append((copy, mine > 0, mine < total - 1))
            else:
                copies.append((copy, mine < total - 1, mine > 0))
        return copies

    def start_halo(window, for_y, for_z, for_x):
        ahead = window % 2 == 0
        at_y, at_z = (0, 0) if ahead else (size_y - 1, size_z - 1)
        for k in range(2):
            send_y[window, k] = for_y[k][at_y]
            send_z[window, k] = for_z[k][:, at_z : at_z + 1, :]
        copies = halo_copies(window)
        for copy, sends, receives in copies[:2]:
            @pl.when(sends)
            def _():
                copy.start()
        packed = jnp.zeros((size_z, LANES), F32)
        for k in range(2):
            for y in range(size_y):
                spot = k * size_y + y
                amount = spot if ahead else (spot + 1) % LANES
                value = for_x[k][y]
                turned = pltpu.roll(value, amount, 1) if amount else value
                packed = jnp.where(lane == spot, turned, packed)
        send_x[window] = packed
        copy, sends, receives = copies[2]

        @pl.when(sends)
        def _():
            copy.start()

    def wait_halo(window):
        for copy, sends, receives in halo_copies(window):
            @pl.when(receives)
            def _():
                copy.wait_recv()

    def inner(ahead, axis, value):
        if axis == 0:
            none = jnp.zeros_like(value[:1])
            if ahead:
                return jnp.concatenate([value[1:], none], axis=0) - value
            return value - jnp.concatenate([none, value[:-1]], axis=0)
        length = value.shape[axis]
        spots = row3 if axis == 1 else lane3
        if ahead:
            return jnp.where(spots == length - 1, 0.0, pltpu.roll(value, length - 1, axis)) - value
        return value - jnp.where(spots == 0, 0.0, pltpu.roll(value, 1, axis))

    def edge_y(window, k):
        other = got_y[window, k][None]
        none = jnp.zeros((size_y - 1, size_z, LANES), F32)
        return jnp.concatenate([none, other] if window % 2 == 0 else [other, none], axis=0)

    def edge_z(window, k):
        return jnp.where(row3 == (size_z - 1 if window % 2 == 0 else 0), got_z[window, k], 0.0)

    def edge_x(window, k):
        landed = got_x[window]
        edges = []
        for y in range(size_y):
            spot = k * size_y + y
            amount = (LANES - 1 - spot) if window % 2 == 0 else (LANES - spot) % LANES
            edges.append(pltpu.roll(landed, amount, 1) if amount else landed)
        return jnp.where(lane3 == (size_x - 1 if window % 2 == 0 else 0), jnp.stack(edges, axis=0), 0.0)

    ex, ey, ez = fields[0], fields[1], fields[2]
    start_halo(0, (ez, ex), (ey, ex), (ez, ey))
    loading[1].wait()
    rate = COURANT / permit[...]
    loading[2].wait()
    hx, hy, hz = fields[3], fields[4], fields[5]
    spec_from = spectra
    for n in range(STEPS):
        window = 2 * n
        hx = hx - COURANT * (inner(True, 0, ez) - inner(True, 1, ey))
        hy = hy - COURANT * (inner(True, 1, ex) - inner(True, 2, ez))
        hz = hz - COURANT * (inner(True, 2, ey) - inner(True, 0, ex))
        tables_of(window)
        wait_halo(window)
        hx = hx - COURANT * (edge_y(window, 0) - edge_z(window, 0))
        hy = hy - COURANT * (edge_z(window, 1) - edge_x(window, 0))
        hz = hz - COURANT * (edge_x(window, 1) - edge_y(window, 1))
        window = 2 * n + 1
        start_halo(window, (hz, hx), (hy, hx), (hz, hy))
        half_c, half_s = run_c[2 * n : 2 * n + 1, :], run_s[2 * n : 2 * n + 1, :]
        for c, value in enumerate((hx, hy, hz)):
            spectra_out[3 + c] = spec_from[3 + c] + value * half_c
            spectra_out[9 + c] = spec_from[9 + c] - value * half_s
        ex = ex + rate * (inner(False, 0, hz) - inner(False, 1, hy))
        ey = ey + rate * (inner(False, 1, hx) - inner(False, 2, hz))
        ez = ez + rate * (inner(False, 2, hy) - inner(False, 0, hx))
        tables_of(window)
        wait_halo(window)
        ex = ex - rate * (edge_y(window, 0) - edge_z(window, 0))
        ey = ey - rate * (edge_z(window, 1) - edge_x(window, 0))
        ez = ez - rate * (edge_x(window, 1) - edge_y(window, 1))
        if n < STEPS - 1:
            start_halo(window + 1, (ez, ex), (ey, ex), (ez, ey))
        full_c, full_s = run_c[2 * n + 1 : 2 * n + 2, :], run_s[2 * n + 1 : 2 * n + 2, :]
        for c, value in enumerate((ex, ey, ez)):
            spectra_out[c] = spec_from[c] + value * full_c
            spectra_out[6 + c] = spec_from[6 + c] - value * full_s
        spec_from = spectra_out
    for c, value in enumerate((ex, ey, ez, hx, hy, hz)):
        fields_out[c] = value

    own_walls = walls.at[gz]
    lane_block = iota((8, LANES), 1) // PATCH
    sub = iota((8, LANES), 0)
    own_block = lane_block == sub
    z_row = iota((size_z, LANES), 0)
    own_walls[...] = jnp.zeros((8, LANES), F32)
    for y in range(size_y):
        spread = jnp.zeros((size_z, LANES), F32)
        for c in range(8):
            k = c % 4
            from_c = X_PICKS[k] + (6 if c >= 4 else 0)
            column = jnp.sum(jnp.where(lane == x_wall, spectra_out[from_c, y], 0.0), axis=1, keepdims=True)
            spread = jnp.where(lane == c * PATCH + z_row, column * (CURRENT_SIGNS[k] * facing_x), spread)
        record = jnp.sum(spread, axis=0, keepdims=True)
        own_walls[pl.ds(y, 1), :] = record
        for c in range(8):
            k = c % 4
            from_c = Z_PICKS[k] + (6 if c >= 4 else 0)
            low = spectra_out[from_c, y, pl.ds(ZB, 1), :]
            high = spectra_out[from_c, y, pl.ds(size_z - 1 - ZB, 1), :]
            picked = jnp.where(gz == 0, low, high) * (CURRENT_SIGNS[k] * facing_z * end_weight)
            cap_plane[pl.ds(8 * y + c, 1), :] = picked
        wall_hi, wall_lo = split(jnp.where(own_block, record, 0.0) * norm)
        cap_hi, cap_lo = split(cap_plane[pl.ds(8 * y, 8), :] * norm)
        none = jnp.zeros((8, LANES), BF16)
        for at, (cap_part, wall_part) in enumerate(((cap_hi, wall_hi), (cap_lo, wall_lo))):
            first = at * all_rows + 8 * y
            lhs[pl.ds(first, 8), :] = jnp.concatenate([cap_part, none], axis=1)
            lhs[pl.ds(first + half_rows, 8), :] = jnp.concatenate([none, wall_part], axis=1)

    lanes8 = iota((1, LANES), 1)
    owner_row = jnp.zeros((1, LANES), F32)
    for p in range(size_y):
        owner_row = jnp.where(lanes8 == 8 * gz + p, (wall_owner[0, p] + 1).astype(F32), owner_row)
    own_walls[pl.ds(size_y, 1), :] = owner_row

    def wall_copy(k):
        return pltpu.make_async_remote_copy(
            src_ref=walls.at[gz],
            dst_ref=walls.at[gz],
            send_sem=wall_send.at[k],
            recv_sem=wall_got.at[gz],
            device_id={"gz": (gz + k) % slabs},
            device_id_type=MESH,
        )

    def wall_landing(s):
        return pltpu.make_async_remote_copy(
            src_ref=walls.at[s], dst_ref=walls.at[s], send_sem=wall_send.at[0], recv_sem=wall_got.at[s],
            device_id={"gz": (gz + 1) % slabs}, device_id_type=MESH,
        )

    def cap_copy(k, at):
        return pltpu.make_async_remote_copy(
            src_ref=caps.at[at],
            dst_ref=caps.at[at],
            send_sem=cap_send.at[k],
            recv_sem=cap_got.at[at],
            device_id={"gz": (gz + k) % slabs},
            device_id_type=MESH,
        )

    for k in range(1, slabs):
        wall_copy(k).start()
    for at, holder in enumerate((0, slabs - 1)):
        @pl.when(gz == holder)
        def _():
            for y in range(size_y):
                caps[at, pl.ds(8 * y, 8), :] = block_transpose(cap_plane[pl.ds(8 * y, 8), :])
            for k in range(1, slabs):
                cap_copy(k, at).start()

    sign = jnp.where(sub < 4, -1.0, 1.0)

    def far_of(j):
        rows = lhs[...]
        by_high = jnp.dot(rows, table_hi[j], preferred_element_type=F32)
        by_low = jnp.dot(rows[:all_rows], table_lo[j], preferred_element_type=F32)
        product = by_high[:all_rows] + by_high[all_rows:] + by_low
        theta = jnp.zeros((8, LANES), F32)
        phi = jnp.zeros((8, LANES), F32)
        for face in range(2):
            sum_c = jnp.zeros((8, LANES), F32)
            sum_s = jnp.zeros((8, LANES), F32)
            for y in range(size_y):
                g = face * size_y + y
                tile = product[8 * g : 8 * g + 8]
                tile = tile[:, :LANES] + sign * pltpu.roll(tile[:, LANES:], 4, 0)
                sum_c = sum_c + tile * phases[j, 0, pl.ds(g, 1), :]
                sum_s = sum_s + tile * phases[j, 1, pl.ds(g, 1), :]
            far = sum_c + sign * pltpu.roll(sum_s, 4, 0)
            theta = theta + weights[j, 2 * face] * far
            phi = phi + weights[j, 2 * face + 1] * far

        def four(values):
            pairs = values + pltpu.roll(values, 7, 0)
            return pairs + pltpu.roll(pairs, 6, 0)

        parts_out[j] = jnp.where(sub % 4 == 1, pltpu.roll(four(phi), 1, 0), four(theta))

    chunk = me // ratio

    bunch = 4 if chunks % 4 == 0 else 1

    def partner(number):
        other, bit = 0, 1
        while bit < chunks:
            other = other + bit * ((chunk // bit + number // bit) % 2)
            bit *= 2
        return other

    def part_copy(k):
        peer = (me + k) % peers
        return pltpu.make_async_remote_copy(
            src_ref=parts_out.at[peer // ratio],
            dst_ref=parts_in.at[k],
            send_sem=part_send.at[k],
            recv_sem=part_got.at[k],
            device_id=ident(peer),
            device_id_type=MESH,
        )

    def each_peer(act):
        def body(k, carry):
            act(k)
            return carry

        lax.fori_loop(1, peers, body, 0)

    def far_and_send(number, carry):
        several = [partner(chunks - 1 - bunch * number - m) for m in range(bunch)]
        for to in several:
            far_of(to)

        def send(m, inner_carry):
            to = partner(chunks - 1 - bunch * number - m // ratio)
            peer = to * ratio + m % ratio

            @pl.when(peer != me)
            def _():
                part_copy((peer - me + peers) % peers).start()

            return inner_carry

        lax.fori_loop(0, bunch * ratio, send, 0)
        return carry

    lax.fori_loop(0, chunks // bunch, far_and_send, 0)
    parts_in[0] = parts_out[chunk]

    for s in range(slabs):
        @pl.when(s != gz)
        def _():
            wall_landing(s).wait_recv()
    for at, holder in enumerate((0, slabs - 1)):
        @pl.when(gz != holder)
        def _():
            cap_copy(1, at).wait_recv()

    def choose(mine, share, records):
        length = mine.shape[1]
        before = jnp.where(iota((length, length), 0) < iota((length, length), 1), 1.0, 0.0).astype(BF16)
        ones = jnp.broadcast_to(jnp.where(mine, 1.0, 0.0), (8, length))
        rank = jnp.dot(ones.astype(BF16), before, preferred_element_type=F32)
        wanted = iota((8, length), 0).astype(F32)
        chooser = jnp.where(rank == wanted, ones, 0.0)
        return jnp.dot(chooser, records, precision=HIGHEST, preferred_element_type=F32)[:share]

    all_walls = walls[...]
    owner_all = jnp.sum(all_walls[:, size_y : size_y + 1, :], axis=0)[:, : 8 * slabs]
    cap_share = (owned_out.shape[0] - size_y) // 2
    owned_out[pl.ds(0, size_y), 0, :] = choose(
        owner_all == (gz + 1).astype(F32), size_y, all_walls.reshape(8 * slabs, LANES)
    )
    for at in range(2):
        owned_out[pl.ds(size_y + at * cap_share, cap_share), 0, :] = choose(
            cap_owner[pl.ds(at, 1), :] == gz, cap_share, caps[at]
        )

    each_peer(lambda k: part_copy(k).wait_recv())
    field = jnp.sum(parts_in[...], axis=0)
    power = jnp.where(sub % 4 < 2, field * field, 0.0)
    intensity = jnp.sum(power, axis=0, keepdims=True)
    intensity_out[...] = intensity
    residual = aim[pl.ds(chunk, 1), :].astype(F32) * (intensity - target[pl.ds(chunk, 1), :])
    leads = me % ratio == 0

    def slope_copy(k, of):
        return pltpu.make_async_remote_copy(
            src_ref=slopes.at[of],
            dst_ref=slopes.at[of],
            send_sem=slope_send.at[k],
            recv_sem=slope_got.at[of],
            device_id=ident((me + k) % peers),
            device_id_type=MESH,
        )

    @pl.when(leads)
    def _():
        slopes[chunk] = 2.0 * residual * field
        each_peer(lambda k: slope_copy(k, chunk).start())

    for window in range(windows):
        for copy, sends, receives in halo_copies(window):
            @pl.when(sends)
            def _():
                copy.wait_send()
    each_peer(lambda k: part_copy(k).wait_send())

    for k in range(1, slabs):
        wall_copy(k).wait_send()
    for at, holder in enumerate((0, slabs - 1)):
        @pl.when(gz == holder)
        def _():
            for k in range(1, slabs):
                cap_copy(k, at).wait_send()

    def adjoint_of(j):
        slope = slopes[j]
        by_theta = jnp.where(sub < 4, slope[0:1], slope[4:5])
        by_phi = jnp.where(sub < 4, slope[1:2], slope[5:6])
        tiles = []
        for face in range(2):
            vector = weights[j, 2 * face] * by_theta + weights[j, 2 * face + 1] * by_phi
            turned = -sign * pltpu.roll(vector, 4, 0)
            for y in range(size_y):
                g = face * size_y + y
                tile = vector * phases[j, 0, pl.ds(g, 1), :] + turned * phases[j, 1, pl.ds(g, 1), :]
                tiles.append(jnp.concatenate([tile, -sign * pltpu.roll(tile, 4, 0)], axis=1))
        rows = jnp.concatenate(tiles, axis=0)
        high, low = split(rows)
        both = jnp.concatenate([high, low], axis=0)
        across = (((1,), (1,)), ((), ()))
        by_high = lax.dot_general(both, table_hi[j], across, preferred_element_type=F32)
        by_low = lax.dot_general(high, table_lo[j], across, preferred_element_type=F32)
        return by_high[:all_rows] + by_high[all_rows:] + by_low

    def adjoint_some(number, total):
        several = [partner(bunch * number + m) for m in range(bunch)]
        for j in several:
            @pl.when(j * ratio != me)
            def _():
                slope_copy(1, j).wait_recv()

        for j in several:
            total = total + adjoint_of(j)
        return total

    gradient = lax.fori_loop(0, chunks // bunch, adjoint_some, jnp.zeros((all_rows, size_x + 8 * size_z), F32))
    for y in range(size_y):
        wall = gradient[half_rows + 8 * y : half_rows + 8 * y + 8, size_x:]
        adjoint_out[pl.ds(y, 1), 0, :] = jnp.sum(jnp.where(own_block, wall, 0.0), axis=0, keepdims=True) * norm
        cap = block_transpose(gradient[8 * y : 8 * y + 8, :size_x] * (norm * end_weight))
        adjoint_out[pl.ds(size_y + 8 * y, 8), 0, :] = cap

    @pl.when(leads)
    def _():
        each_peer(lambda k: slope_copy(k, chunk).wait_send())


def write_out(*refs):
    copies = [pltpu.make_async_copy(refs[i], refs[5 + i], refs[10].at[i]) for i in range(5)]
    for copy in copies:
        copy.start()
    for copy in copies:
        copy.wait()


def local(fields, spectra, permittivity, phase_start, wall_owner, cap_owner, dir_index, target, aim_mask):
    slabs, devs, xys = (lax.axis_size(a) for a in ("gz", "dev", "xy"))
    peers = slabs * devs * xys
    size_y, size_z, size_x = permittivity.shape
    assert size_z == PATCH and size_x == LANES and size_y == 4
    directions = dir_index.shape[0]
    chunks = directions // LANES
    ratio = peers // chunks
    share = directions // peers
    cap_count = size_y * size_x // PATCH
    owned = size_y + 2 * (cap_count // slabs)
    rows = 16 * size_y
    depth = size_x + 8 * size_z
    windows = 2 * STEPS
    vmem, smem = (pl.BlockSpec(memory_space=s) for s in (pltpu.VMEM, pltpu.SMEM))
    anywhere = pl.BlockSpec(memory_space=pl.ANY)
    dma = pltpu.SemaphoreType.DMA
    outs = pl.pallas_call(
        functools.partial(kernel, (slabs, devs, xys)),
        out_shape=(
            pltpu.VMEM(fields.shape, F32),
            pltpu.VMEM(spectra.shape, F32),
            pltpu.VMEM((owned, 1, LANES), F32),
            pltpu.VMEM((1, LANES), F32),
            pltpu.VMEM((size_y + cap_count, 1, LANES), F32),
        ),
        in_specs=[anywhere, anywhere, anywhere, vmem, smem, vmem, vmem, vmem, vmem],
        out_specs=(vmem,) * 5,
        scratch_shapes=[
            pltpu.VMEM((windows, 2, size_z, LANES), F32),
            pltpu.VMEM((windows, 2, size_y, 1, LANES), F32),
            pltpu.VMEM((windows, size_z, LANES), F32),
            pltpu.VMEM((windows, 2, size_z, LANES), F32),
            pltpu.VMEM((windows, 2, size_y, 1, LANES), F32),
            pltpu.VMEM((windows, size_z, LANES), F32),
            pltpu.VMEM(fields.shape, F32),
            pltpu.VMEM(spectra.shape, F32),
            pltpu.VMEM(permittivity.shape, F32),
            pltpu.VMEM((8, chunks, LANES), F32),
            pltpu.VMEM((chunks, 4, 8, LANES), F32),
            pltpu.VMEM((chunks, 2, 2 * size_y, LANES), F32),
            pltpu.VMEM((chunks, depth, 2 * LANES), BF16),
            pltpu.VMEM((chunks, depth, 2 * LANES), BF16),
            pltpu.VMEM((8 * size_y, LANES), F32),
            pltpu.VMEM((2 * rows, depth), BF16),
            pltpu.VMEM((chunks, 8, LANES), F32),
            pltpu.VMEM((peers, 8, LANES), F32),
            pltpu.VMEM((chunks, 8, LANES), F32),
            pltpu.VMEM((slabs, 8, LANES), F32),
            pltpu.VMEM((2, cap_count, LANES), F32),
            dma((windows, 3)), dma((windows, 3)),
            dma((peers,)), dma((peers,)),
            dma((peers,)), dma((chunks,)),
            dma((slabs,)), dma((slabs,)),
            dma((slabs,)), dma((2,)),
            dma((3,)),
        ],
        compiler_params=pltpu.CompilerParams(collective_id=0, has_side_effects=True),
    )(
        fields, spectra, permittivity, phase_start.reshape(1, 1), wall_owner, cap_owner,
        dir_index.reshape(chunks, LANES), target.reshape(chunks, LANES), aim_mask.reshape(chunks, LANES),
    )
    held = (fields.shape, spectra.shape, (owned, 1, LANES), (1, LANES), (size_y + cap_count, 1, LANES))
    fields_new, spectra_new, owned_rows, intensity, adjoint = pl.pallas_call(
        write_out,
        out_shape=tuple(jax.ShapeDtypeStruct(shape, F32) for shape in held),
        in_specs=[pl.BlockSpec(memory_space=pltpu.VMEM)] * 5,
        out_specs=(pl.BlockSpec(memory_space=pl.ANY),) * 5,
        scratch_shapes=[dma((5,))],
    )(*(pltpu.with_memory_space_constraint(out, pltpu.VMEM) for out in outs))
    owned_rows = owned_rows.reshape(1, 1, owned, 1, LANES).transpose(0, 1, 3, 2, 4)
    adjoint = adjoint.reshape(1, 1, size_y + cap_count, 1, LANES).transpose(0, 1, 3, 2, 4)
    intensity = intensity.reshape(LANES)
    if ratio > 1:
        me = (lax.axis_index("gz") * devs + lax.axis_index("dev")) * xys + lax.axis_index("xy")
        intensity = lax.dynamic_slice_in_dim(intensity, (me % ratio) * share, share, 0)
    return (fields_new, spectra_new, owned_rows, intensity, adjoint)


def solution(mesh):
    placed = (
        P("groups", "dev", "gz", "xy"),
        P("groups", "dev", "gz", "xy"),
        P(("groups", "dev"), "gz", "xy"),
        P("groups"),
        P("gz", None),
        P(),
        P(),
        P("groups"),
        P("groups"),
    )
    return jax.shard_map(
        local,
        mesh=mesh,
        in_specs=placed,
        out_specs=(
            P("groups", "dev", "gz", "xy"),
            P("groups", "dev", "gz", "xy"),
            P(("groups", "gz"), "dev", "xy", None, None),
            P(("groups", "gz", "dev", "xy")),
            P(("groups", "gz"), "dev", "xy", None, None),
        ),
        check_vma=False,
    )
```

profile of v0, /device:TPU:0, one launch (start us, length us, event | category | flops | bytes accessed | tf_op | source)
XLA Modules:
  0.0 36.6 jit_solution(6658765444113564900)
XLA Ops:
  1.3 34.5 %shard_map.128 = (f32[6,4,16,128]{3,2,1,0:T(8,128)S(1)}, f32[12,4,16,128]{3,2,1,0:T(8,128)S(1)}, f32[20,1,128]{2,1,0:T(1,128)S(1)}, f32[1,128]{1,0:T(1,128)S(1)}, f32[36,1,128]{2,1,0:T(1,128)S(1)}) custom-call(f32[6,4,16,128]{3,2,1,0:T(8,128)} %fields_in.1, f32[12,4,16,128]{3,2,1,0:T(8,128)} %spectra_in.1, f32[4,16,128]{2,1,0:T(8,128)} %permit_in.1, ...), custom_call_target="tpu_custom_call" | custom-call | tf_op jit(solution)/shard_map/pallas_call | solution.py:592
  35.8 0.9 %shard_map.129 = (f32[6,4,16,128]{3,2,1,0:T(8,128)}, f32[12,4,16,128]{3,2,1,0:T(8,128)}, f32[20,1,128]{2,1,0:T(1,128)}, f32[1,128]{1,0:T(1,128)}, f32[36,1,128]{2,1,0:T(1,128)}) custom-call(f32[6,4,16,128]{3,2,1,0:T(8,128)S(1)} %get-tuple-element.15.refs_0_, f32[12,4,16,128]{3,2,1,0:T(8,128)S(1)} %get-tuple-element.16.refs_1_, ...), custom_call_target="tpu_custom_call" | custom-call | tf_op jit(solution)/shard_map/pallas_call | solution.py:638
where the time goes:
time: 36.9 us; the launch traced here: 36.6 us
  Pallas kernels  35.4 us (96%)
  between operations  1.29 us (3%)
    pallas_call x1, Pallas kernels, local(): pl.pallas_call(functools.partial(kernel, (slabs, devs, xys)), out_shape=(...  34.5 us
    pallas_call x1, Pallas kernels, local(): pl.pallas_call(write_out, out_shape=tuple((jax.ShapeDtypeStruct(shape, F3...  0.86 us

commit v1 on v0

--- a/solution.py
+++ b/solution.py
@@ -55,18 +55,22 @@
 
 def kernel(
     sizes,
-    fields_in, spectra_in, permit_in, phase, wall_owner, cap_owner, dirs, target, aim,
+    fields_in, spectra_in, permit_in, phase_in, wall_owner_in, cap_owner_in, dirs_in, target_in, aim_in,
     fields_out, spectra_out, owned_out, intensity_out, adjoint_out,
     send_y, send_z, send_x, got_y, got_z, got_x,
-    fields, spectra, permit, geo, weights, phases, table_hi, table_lo, cap_plane, lhs,
-    parts_out, parts_in, slopes, walls, caps,
-    halo_send, halo_got, part_send, part_got, slope_send, slope_got, wall_send, wall_got, cap_send, cap_got, loads,
+    fields, spectra, permit, phase, wall_owner, cap_owner, dirs, target, aim,
+    geo, weights, phases, table_hi, table_lo, cap_plane, lhs,
+    parts_out, parts_in, totals, walls, caps,
+    halo_send, halo_got, part_send, part_got, total_send, total_got, wall_send, wall_got, cap_send, cap_got, loads,
 ):
     slabs, devs, xys = sizes
     peers = slabs * devs * xys
     size_y, size_z, size_x = permit.shape
     chunks = dirs.shape[0]
     ratio = peers // chunks
+    across = devs * xys
+    per = max(1, chunks // (2 * across))
+    owners = chunks // per
     groups = 2 * size_y
     half_rows = 8 * size_y
     all_rows = 2 * half_rows
@@ -75,24 +79,29 @@
     place = {"dev": dev, "gz": gz, "xy": xy}
     count = {"dev": devs, "gz": slabs, "xy": xys}
 
+    def ident(flat):
+        return {"gz": flat // (devs * xys), "dev": (flat // xys) % devs, "xy": flat % xys}
+
+    barrier = pltpu.get_barrier_semaphore()
+
+    def greet(k, carry):
+        pl.semaphore_signal(barrier, inc=1, device_id=ident((me + k) % peers), device_id_type=MESH)
+        return carry
+
+    lax.fori_loop(1, peers, greet, 0)
+
     loading = [
         pltpu.make_async_copy(source, held, loads.at[number])
-        for number, (source, held) in enumerate(((fields_in, fields), (permit_in, permit), (spectra_in, spectra)))
+        for number, (source, held) in enumerate((
+            (fields_in, fields), (dirs_in, dirs), (phase_in, phase), (permit_in, permit), (spectra_in, spectra),
+            (wall_owner_in, wall_owner), (cap_owner_in, cap_owner), (target_in, target), (aim_in, aim),
+        ))
     ]
     for copy in loading:
         copy.start()
 
-    def ident(flat):
-        return {"gz": flat // (devs * xys), "dev": (flat // xys) % devs, "xy": flat % xys}
-
-    barrier = pltpu.get_barrier_semaphore()
-
-    def greet(k, carry):
-        pl.semaphore_signal(barrier, inc=1, device_id=ident((me + k) % peers), device_id_type=MESH)
-        return carry
-
-    lax.fori_loop(1, peers, greet, 0)
-
+    for copy in loading[1:3]:
+        copy.wait()
     index = dirs[...]
     sin_t, cos_t = sincos(((index // THETAS).astype(F32) + 0.5) * (0.5 / THETAS))
     sin_f, cos_f = sincos((index % THETAS).astype(F32) * (1.0 / THETAS))
@@ -161,7 +170,7 @@
         lax.fori_loop(window * chunks // windows, (window + 1) * chunks // windows, make_tables, 0)
 
     order = iota((8, LANES), 0).astype(F32)
-    run_s, run_c = sincos((phase[...] + 0.5 * ANGULAR_STEP * (order + 1.0)) * (0.5 / math.pi))
+    run_s, run_c = sincos((phase[0] + 0.5 * ANGULAR_STEP * (order + 1.0)) * (0.5 / math.pi))
 
     for number, (axis, got) in enumerate(zip(AXES, (got_y, got_z, got_x))):
         @pl.when(place[axis] == count[axis] - 1)
@@ -265,9 +274,10 @@
 
     ex, ey, ez = fields[0], fields[1], fields[2]
     start_halo(0, (ez, ex), (ey, ex), (ez, ey))
-    loading[1].wait()
+    loading[3].wait()
     rate = COURANT / permit[...]
-    loading[2].wait()
+    for copy in loading[4:]:
+        copy.wait()
     hx, hy, hz = fields[3], fields[4], fields[5]
     spec_from = spectra
     for n in range(STEPS):
@@ -366,16 +376,6 @@
             device_id_type=MESH,
         )
 
-    for k in range(1, slabs):
-        wall_copy(k).start()
-    for at, holder in enumerate((0, slabs - 1)):
-        @pl.when(gz == holder)
-        def _():
-            for y in range(size_y):
-                caps[at, pl.ds(8 * y, 8), :] = block_transpose(cap_plane[pl.ds(8 * y, 8), :])
-            for k in range(1, slabs):
-                cap_copy(k, at).start()
-
     sign = jnp.where(sub < 4, -1.0, 1.0)
 
     def far_of(j):
@@ -402,29 +402,60 @@
             pairs = values + pltpu.roll(values, 7, 0)
             return pairs + pltpu.roll(pairs, 6, 0)
 
-        parts_out[j] = jnp.where(sub % 4 == 1, pltpu.roll(four(phi), 1, 0), four(theta))
-
-    chunk = me // ratio
-
-    bunch = 4 if chunks % 4 == 0 else 1
+        both = jnp.where(sub % 4 == 1, pltpu.roll(four(phi), 1, 0), four(theta))
+        parts_out[j] = jnp.where(sub < 2, both, pltpu.roll(both, 6, 0))[:4]
+
+    bunch = per * max(1, 4 // per)
+    together = bunch // per
+    upper = jnp.where(gz >= slabs // 2, 1, 0)
+    near = (upper * across + dev * xys + xy) % owners
 
     def partner(number):
         other, bit = 0, 1
-        while bit < chunks:
-            other = other + bit * ((chunk // bit + number // bit) % 2)
+        while bit < owners:
+            other = other + bit * ((near // bit + number // bit) % 2)
             bit *= 2
         return other
 
-    def part_copy(k):
-        peer = (me + k) % peers
+    def flat_of(owner):
+        return (slabs // 2 - 1) * across + owner
+
+    def part_copy(owner, source):
         return pltpu.make_async_remote_copy(
-            src_ref=parts_out.at[peer // ratio],
-            dst_ref=parts_in.at[k],
-            send_sem=part_send.at[k],
-            recv_sem=part_got.at[k],
-            device_id=ident(peer),
+            src_ref=parts_out.at[pl.ds(owner * per, per)],
+            dst_ref=parts_in.at[source],
+            send_sem=part_send.at[owner],
+            recv_sem=part_got.at[source],
+            device_id=ident(flat_of(owner)),
             device_id_type=MESH,
         )
+
+    mine = me - flat_of(0)
+    leads = jnp.logical_and(mine >= 0, mine < owners)
+
+    def far_and_send(number, carry):
+        several = [partner(owners - 1 - together * number - m) for m in range(together)]
+        for owner in several:
+            for m in range(per):
+                far_of(owner * per + m)
+        for owner in several:
+            @pl.when(owner != mine)
+            def _():
+                part_copy(owner, me).start()
+
+        return carry
+
+    lax.fori_loop(0, owners // together, far_and_send, 0)
+
+    for k in range(1, slabs):
+        wall_copy(k).start()
+    for at, holder in enumerate((0, slabs - 1)):
+        @pl.when(gz == holder)
+        def _():
+            for y in range(size_y):
+                caps[at, pl.ds(8 * y, 8), :] = block_transpose(cap_plane[pl.ds(8 * y, 8), :])
+            for k in range(1, slabs):
+                cap_copy(k, at).start()
 
     def each_peer(act):
         def body(k, carry):
@@ -433,35 +464,22 @@
 
         lax.fori_loop(1, peers, body, 0)
 
-    def far_and_send(number, carry):
-        several = [partner(chunks - 1 - bunch * number - m) for m in range(bunch)]
-        for to in several:
-            far_of(to)
-
-        def send(m, inner_carry):
-            to = partner(chunks - 1 - bunch * number - m // ratio)
-            peer = to * ratio + m % ratio
-
-            @pl.when(peer != me)
-            def _():
-                part_copy((peer - me + peers) % peers).start()
-
-            return inner_carry
-
-        lax.fori_loop(0, bunch * ratio, send, 0)
-        return carry
-
-    lax.fori_loop(0, chunks // bunch, far_and_send, 0)
-    parts_in[0] = parts_out[chunk]
-
-    for s in range(slabs):
-        @pl.when(s != gz)
-        def _():
-            wall_landing(s).wait_recv()
-    for at, holder in enumerate((0, slabs - 1)):
-        @pl.when(gz != holder)
-        def _():
-            cap_copy(1, at).wait_recv()
+    def total_copy(k, owner):
+        return pltpu.make_async_remote_copy(
+            src_ref=totals.at[pl.ds(owner * per, per)],
+            dst_ref=totals.at[pl.ds(owner * per, per)],
+            send_sem=total_send.at[k],
+            recv_sem=total_got.at[owner],
+            device_id=ident((me + k) % peers),
+            device_id_type=MESH,
+        )
+
+    @pl.when(leads)
+    def _():
+        parts_in[me] = parts_out[pl.ds(mine * per, per)]
+        each_peer(lambda k: part_copy(0, (me + k) % peers).wait_recv())
+        totals[pl.ds(mine * per, per)] = jnp.sum(parts_in[...], axis=0)
+        each_peer(lambda k: total_copy(peers - k, mine).start())
 
     def choose(mine, share, records):
         length = mine.shape[1]
@@ -472,59 +490,38 @@
         chooser = jnp.where(rank == wanted, ones, 0.0)
         return jnp.dot(chooser, records, precision=HIGHEST, preferred_element_type=F32)[:share]
 
-    all_walls = walls[...]
-    owner_all = jnp.sum(all_walls[:, size_y : size_y + 1, :], axis=0)[:, : 8 * slabs]
-    cap_share = (owned_out.shape[0] - size_y) // 2
-    owned_out[pl.ds(0, size_y), 0, :] = choose(
-        owner_all == (gz + 1).astype(F32), size_y, all_walls.reshape(8 * slabs, LANES)
-    )
-    for at in range(2):
-        owned_out[pl.ds(size_y + at * cap_share, cap_share), 0, :] = choose(
-            cap_owner[pl.ds(at, 1), :] == gz, cap_share, caps[at]
+    def choose_owned():
+        for s in range(slabs):
+            @pl.when(s != gz)
+            def _():
+                wall_landing(s).wait_recv()
+        for at, holder in enumerate((0, slabs - 1)):
+            @pl.when(gz != holder)
+            def _():
+                cap_copy(1, at).wait_recv()
+        all_walls = walls[...]
+        owner_all = jnp.sum(all_walls[:, size_y : size_y + 1, :], axis=0)[:, : 8 * slabs]
+        cap_share = (owned_out.shape[0] - size_y) // 2
+        owned_out[pl.ds(0, size_y), 0, :] = choose(
+            owner_all == (gz + 1).astype(F32), size_y, all_walls.reshape(8 * slabs, LANES)
         )
-
-    each_peer(lambda k: part_copy(k).wait_recv())
-    field = jnp.sum(parts_in[...], axis=0)
-    power = jnp.where(sub % 4 < 2, field * field, 0.0)
-    intensity = jnp.sum(power, axis=0, keepdims=True)
-    intensity_out[...] = intensity
-    residual = aim[pl.ds(chunk, 1), :].astype(F32) * (intensity - target[pl.ds(chunk, 1), :])
-    leads = me % ratio == 0
-
-    def slope_copy(k, of):
-        return pltpu.make_async_remote_copy(
-            src_ref=slopes.at[of],
-            dst_ref=slopes.at[of],
-            send_sem=slope_send.at[k],
-            recv_sem=slope_got.at[of],
-            device_id=ident((me + k) % peers),
-            device_id_type=MESH,
-        )
-
-    @pl.when(leads)
-    def _():
-        slopes[chunk] = 2.0 * residual * field
-        each_peer(lambda k: slope_copy(k, chunk).start())
-
-    for window in range(windows):
-        for copy, sends, receives in halo_copies(window):
-            @pl.when(sends)
-            def _():
-                copy.wait_send()
-    each_peer(lambda k: part_copy(k).wait_send())
-
-    for k in range(1, slabs):
-        wall_copy(k).wait_send()
-    for at, holder in enumerate((0, slabs - 1)):
-        @pl.when(gz == holder)
-        def _():
-            for k in range(1, slabs):
-                cap_copy(k, at).wait_send()
+        for at in range(2):
+            owned_out[pl.ds(size_y + at * cap_share, cap_share), 0, :] = choose(
+                cap_owner[pl.ds(at, 1), :] == gz, cap_share, caps[at]
+            )
+
+    def intensity_of(field):
+        return jnp.sum(field * field, axis=0, keepdims=True)
+
+    def slope_of(j):
+        field = totals[j]
+        residual = aim[pl.ds(j, 1), :].astype(F32) * (intensity_of(field) - target[pl.ds(j, 1), :])
+        return 2.0 * residual * field
 
     def adjoint_of(j):
-        slope = slopes[j]
-        by_theta = jnp.where(sub < 4, slope[0:1], slope[4:5])
-        by_phi = jnp.where(sub < 4, slope[1:2], slope[5:6])
+        slope = slope_of(j)
+        by_theta = jnp.where(sub < 4, slope[0:1], slope[2:3])
+        by_phi = jnp.where(sub < 4, slope[1:2], slope[3:4])
         tiles = []
         for face in range(2):
             vector = weights[j, 2 * face] * by_theta + weights[j, 2 * face + 1] * by_phi
@@ -542,26 +539,53 @@
         return by_high[:all_rows] + by_high[all_rows:] + by_low
 
     def adjoint_some(number, total):
-        several = [partner(bunch * number + m) for m in range(bunch)]
-        for j in several:
-            @pl.when(j * ratio != me)
+        several = [partner(together * number + m) for m in range(together)]
+        for owner in several:
+            @pl.when(owner != mine)
             def _():
-                slope_copy(1, j).wait_recv()
-
-        for j in several:
-            total = total + adjoint_of(j)
+                total_copy(1, owner).wait_recv()
+
+        for owner in several:
+            for m in range(per):
+                total = total + adjoint_of(owner * per + m)
         return total
 
-    gradient = lax.fori_loop(0, chunks // bunch, adjoint_some, jnp.zeros((all_rows, size_x + 8 * size_z), F32))
+    rounds = owners // together
+    gradient = lax.fori_loop(0, rounds // 2, adjoint_some, jnp.zeros((all_rows, size_x + 8 * size_z), F32))
+    choose_owned()
+    gradient = lax.fori_loop(rounds // 2, rounds, adjoint_some, gradient)
+    intensity_out[...] = intensity_of(totals[me // ratio])
     for y in range(size_y):
         wall = gradient[half_rows + 8 * y : half_rows + 8 * y + 8, size_x:]
         adjoint_out[pl.ds(y, 1), 0, :] = jnp.sum(jnp.where(own_block, wall, 0.0), axis=0, keepdims=True) * norm
         cap = block_transpose(gradient[8 * y : 8 * y + 8, :size_x] * (norm * end_weight))
         adjoint_out[pl.ds(size_y + 8 * y, 8), 0, :] = cap
 
+    for window in range(windows):
+        for copy, sends, receives in halo_copies(window):
+            @pl.when(sends)
+            def _():
+                copy.wait_send()
+
+    def part_sent(owner, carry):
+        @pl.when(owner != mine)
+        def _():
+            part_copy(owner, me).wait_send()
+
+        return carry
+
+    lax.fori_loop(0, owners, part_sent, 0)
+    for k in range(1, slabs):
+        wall_copy(k).wait_send()
+    for at, holder in enumerate((0, slabs - 1)):
+        @pl.when(gz == holder)
+        def _():
+            for k in range(1, slabs):
+                cap_copy(k, at).wait_send()
+
     @pl.when(leads)
     def _():
-        each_peer(lambda k: slope_copy(k, chunk).wait_send())
+        each_peer(lambda k: total_copy(k, mine).wait_send())
 
 
 def write_out(*refs):
@@ -580,13 +604,15 @@
     directions = dir_index.shape[0]
     chunks = directions // LANES
     ratio = peers // chunks
+    per = max(1, chunks // (2 * devs * xys))
+    owners = chunks // per
     share = directions // peers
     cap_count = size_y * size_x // PATCH
     owned = size_y + 2 * (cap_count // slabs)
     rows = 16 * size_y
     depth = size_x + 8 * size_z
     windows = 2 * STEPS
-    vmem, smem = (pl.BlockSpec(memory_space=s) for s in (pltpu.VMEM, pltpu.SMEM))
+    vmem = pl.BlockSpec(memory_space=pltpu.VMEM)
     anywhere = pl.BlockSpec(memory_space=pl.ANY)
     dma = pltpu.SemaphoreType.DMA
     outs = pl.pallas_call(
@@ -598,7 +624,7 @@
             pltpu.VMEM((1, LANES), F32),
             pltpu.VMEM((size_y + cap_count, 1, LANES), F32),
         ),
-        in_specs=[anywhere, anywhere, anywhere, vmem, smem, vmem, vmem, vmem, vmem],
+        in_specs=[anywhere] * 9,
         out_specs=(vmem,) * 5,
         scratch_shapes=[
             pltpu.VMEM((windows, 2, size_z, LANES), F32),
@@ -610,6 +636,12 @@
             pltpu.VMEM(fields.shape, F32),
             pltpu.VMEM(spectra.shape, F32),
             pltpu.VMEM(permittivity.shape, F32),
+            pltpu.SMEM((1,), F32),
+            pltpu.SMEM(wall_owner.shape, jnp.int32),
+            pltpu.VMEM(cap_owner.shape, jnp.int32),
+            pltpu.VMEM((chunks, LANES), jnp.int32),
+            pltpu.VMEM((chunks, LANES), F32),
+            pltpu.VMEM((chunks, LANES), jnp.int32),
             pltpu.VMEM((8, chunks, LANES), F32),
             pltpu.VMEM((chunks, 4, 8, LANES), F32),
             pltpu.VMEM((chunks, 2, 2 * size_y, LANES), F32),
@@ -617,21 +649,21 @@
             pltpu.VMEM((chunks, depth, 2 * LANES), BF16),
             pltpu.VMEM((8 * size_y, LANES), F32),
             pltpu.VMEM((2 * rows, depth), BF16),
-            pltpu.VMEM((chunks, 8, LANES), F32),
-            pltpu.VMEM((peers, 8, LANES), F32),
-            pltpu.VMEM((chunks, 8, LANES), F32),
+            pltpu.VMEM((chunks, 4, LANES), F32),
+            pltpu.VMEM((peers, per, 4, LANES), F32),
+            pltpu.VMEM((chunks, 4, LANES), F32),
             pltpu.VMEM((slabs, 8, LANES), F32),
             pltpu.VMEM((2, cap_count, LANES), F32),
             dma((windows, 3)), dma((windows, 3)),
-            dma((peers,)), dma((peers,)),
-            dma((peers,)), dma((chunks,)),
+            dma((owners,)), dma((peers,)),
+            dma((peers,)), dma((owners,)),
             dma((slabs,)), dma((slabs,)),
             dma((slabs,)), dma((2,)),
-            dma((3,)),
+            dma((9,)),
         ],
         compiler_params=pltpu.CompilerParams(collective_id=0, has_side_effects=True),
     )(
-        fields, spectra, permittivity, phase_start.reshape(1, 1), wall_owner, cap_owner,
+        fields, spectra, permittivity, phase_start, wall_owner, cap_owner,
         dir_index.reshape(chunks, LANES), target.reshape(chunks, LANES), aim_mask.reshape(chunks, LANES),
     )
     held = (fields.shape, spectra.shape, (owned, 1, LANES), (1, LANES), (size_y + cap_count, 1, LANES))

time: 36.9 us -> 35.5 us (0.962)
  Pallas kernels: 35.4 us -> 34 us
    pallas_call x1, Pallas kernels: 34.5 us -> 33.2 us  [local(): pl.pallas_call(functools.partial(kernel, (slabs, devs, xys)), out_shape=(...]
where the time goes in v1:
time: 35.5 us; the launch traced here: 35.3 us
  Pallas kernels  34 us (96%)
  between operations  1.29 us (4%)
    pallas_call x1, Pallas kernels, local(): pl.pallas_call(functools.partial(kernel, (slabs, devs, xys)), out_shape=(...  33.2 us
    pallas_call x1, Pallas kernels, local(): pl.pallas_call(write_out, out_shape=tuple((jax.ShapeDtypeStruct(shape, F3...  0.86 us

profile of v1, /device:TPU:0, one launch (start us, length us, event | category | flops | bytes accessed | tf_op | source)
XLA Modules:
  0.0 35.3 jit_solution(3979675382557908039)
XLA Ops:
  1.3 33.2 %shard_map.128 = (f32[6,4,16,128]{3,2,1,0:T(8,128)S(1)}, f32[12,4,16,128]{3,2,1,0:T(8,128)S(1)}, f32[20,1,128]{2,1,0:T(1,128)S(1)}, f32[1,128]{1,0:T(1,128)S(1)}, f32[36,1,128]{2,1,0:T(1,128)S(1)}) custom-call(f32[6,4,16,128]{3,2,1,0:T(8,128)} %fields_in.1, f32[12,4,16,128]{3,2,1,0:T(8,128)} %spectra_in.1, f32[4,16,128]{2,1,0:T(8,128)} %permit_in.1, ...), custom_call_target="tpu_custom_call" | custom-call | tf_op jit(solution)/shard_map/pallas_call | solution.py:618
  34.5 0.9 %shard_map.129 = (f32[6,4,16,128]{3,2,1,0:T(8,128)}, f32[12,4,16,128]{3,2,1,0:T(8,128)}, f32[20,1,128]{2,1,0:T(1,128)}, f32[1,128]{1,0:T(1,128)}, f32[36,1,128]{2,1,0:T(1,128)}) custom-call(f32[6,4,16,128]{3,2,1,0:T(8,128)S(1)} %get-tuple-element.15.refs_0_, f32[12,4,16,128]{3,2,1,0:T(8,128)S(1)} %get-tuple-element.16.refs_1_, ...), custom_call_target="tpu_custom_call" | custom-call | tf_op jit(solution)/shard_map/pallas_call | solution.py:670

commit v2 on v1

--- a/solution.py
+++ b/solution.py
@@ -57,11 +57,12 @@
     sizes,
     fields_in, spectra_in, permit_in, phase_in, wall_owner_in, cap_owner_in, dirs_in, target_in, aim_in,
     fields_out, spectra_out, owned_out, intensity_out, adjoint_out,
-    send_y, send_z, send_x, got_y, got_z, got_x,
+    out_yu, out_yd, out_zu, out_zd, out_xu, out_xd,
+    in_yu, in_yd, in_zu, in_zd, in_xu, in_xd, in_zy, in_yz, in_yx, in_zx, in_xz, in_xy,
     fields, spectra, permit, phase, wall_owner, cap_owner, dirs, target, aim,
     geo, weights, phases, table_hi, table_lo, cap_plane, lhs,
     parts_out, parts_in, totals, walls, caps,
-    halo_send, halo_got, part_send, part_got, total_send, total_got, wall_send, wall_got, cap_send, cap_got, loads,
+    halo_send, halo_got, part_send, part_got, total_send, total_got, wall_send, wall_got, cap_send, cap_got, loads, chain,
 ):
     slabs, devs, xys = sizes
     peers = slabs * devs * xys
@@ -84,11 +85,31 @@
 
     barrier = pltpu.get_barrier_semaphore()
 
-    def greet(k, carry):
-        pl.semaphore_signal(barrier, inc=1, device_id=ident((me + k) % peers), device_id_type=MESH)
-        return carry
-
-    lax.fori_loop(1, peers, greet, 0)
+    for away in (1, -1, 0):
+        @pl.when(jnp.logical_and(gz + away >= 0, gz + away < slabs))
+        def _():
+            def greet(k, carry):
+                spot = (dev * xys + xy + k) % across
+                to = {"gz": gz + away, "dev": spot // xys, "xy": spot % xys}
+                pl.semaphore_signal(barrier, inc=1, device_id=to, device_id_type=MESH)
+                return carry
+
+            lax.fori_loop(0 if away else 1, across, greet, 0)
+
+    beside = jnp.where(gz > 0, across, 0) + jnp.where(gz < slabs - 1, across, 0) + across - 1
+
+    def pass_on():
+        for at, away in enumerate((1, -1)):
+            @pl.when(jnp.logical_and(gz + away >= 0, gz + away < slabs))
+            def _():
+                to = {"gz": gz + away, "dev": dev, "xy": xy}
+                pl.semaphore_signal(chain.at[at], inc=1, device_id=to, device_id_type=MESH)
+
+    def hear():
+        for at, away in enumerate((1, -1)):
+            @pl.when(jnp.logical_and(gz - away >= 0, gz - away < slabs))
+            def _():
+                pl.semaphore_wait(chain.at[at], 1)
 
     loading = [
         pltpu.make_async_copy(source, held, loads.at[number])
@@ -100,17 +121,16 @@
     for copy in loading:
         copy.start()
 
-    for copy in loading[1:3]:
-        copy.wait()
-    index = dirs[...]
-    sin_t, cos_t = sincos(((index // THETAS).astype(F32) + 0.5) * (0.5 / THETAS))
-    sin_f, cos_f = sincos((index % THETAS).astype(F32) * (1.0 / THETAS))
-    wave = WAVE_NUMBER / (2.0 * math.pi)
-    for slot, values in enumerate((
-        wave * sin_t * cos_f, wave * sin_t * sin_f, wave * cos_t,
-        cos_t * cos_f, cos_t * sin_f, -sin_t, -sin_f, cos_f,
-    )):
-        geo[slot] = values
+    def geometry():
+        index = dirs[...]
+        sin_t, cos_t = sincos(((index // THETAS).astype(F32) + 0.5) * (0.5 / THETAS))
+        sin_f, cos_f = sincos((index % THETAS).astype(F32) * (1.0 / THETAS))
+        wave = WAVE_NUMBER / (2.0 * math.pi)
+        for slot, values in enumerate((
+            wave * sin_t * cos_f, wave * sin_t * sin_f, wave * cos_t,
+            cos_t * cos_f, cos_t * sin_f, -sin_t, -sin_f, cos_f,
+        )):
+            geo[slot] = values
 
     grid_x, grid_y, grid_z = size_x * xys, size_y * devs, size_z * slabs
     x_first = (xy * size_x).astype(F32) - (grid_x - 1) / 2.0
@@ -164,84 +184,98 @@
         weights[j, 3] = pattern(-fy, jnp.zeros_like(fy), ty, tz)
         return carry
 
-    windows = 2 * STEPS
+    windows = STEPS
 
     def tables_of(window):
         lax.fori_loop(window * chunks // windows, (window + 1) * chunks // windows, make_tables, 0)
-
-    order = iota((8, LANES), 0).astype(F32)
-    run_s, run_c = sincos((phase[0] + 0.5 * ANGULAR_STEP * (order + 1.0)) * (0.5 / math.pi))
-
-    for number, (axis, got) in enumerate(zip(AXES, (got_y, got_z, got_x))):
-        @pl.when(place[axis] == count[axis] - 1)
-        def _():
-            for window in range(0, windows, 2):
-                got[window] = jnp.zeros(got.shape[1:], F32)
-
-        @pl.when(place[axis] == 0)
-        def _():
-            for window in range(1, windows, 2):
-                got[window] = jnp.zeros(got.shape[1:], F32)
-
-    loading[0].wait()
-    pl.semaphore_wait(barrier, peers - 1)
 
     lane = iota((size_z, LANES), 1)
     lane3 = iota((size_y, size_z, LANES), 2)
     row3 = iota((size_y, size_z, LANES), 1)
 
-    def halo_copies(window):
-        step = -1 if window % 2 == 0 else 1
-        copies = []
-        for number, (axis, source, landing) in enumerate(
-            zip(AXES, (send_y, send_z, send_x), (got_y, got_z, got_x))
-        ):
-            mine, total = place[axis], count[axis]
-            copy = pltpu.make_async_remote_copy(
-                src_ref=source.at[window],
-                dst_ref=landing.at[window],
-                send_sem=halo_send.at[window, number],
-                recv_sem=halo_got.at[window, number],
-                device_id={axis: (mine + step + total) % total},
-                device_id_type=MESH,
-            )
-            if step < 0:
-                copies.append((copy, mine > 0, mine < total - 1))
-            else:
-                copies.append((copy, mine < total - 1, mine > 0))
-        return copies
-
-    def start_halo(window, for_y, for_z, for_x):
-        ahead = window % 2 == 0
-        at_y, at_z = (0, 0) if ahead else (size_y - 1, size_z - 1)
-        for k in range(2):
-            send_y[window, k] = for_y[k][at_y]
-            send_z[window, k] = for_z[k][:, at_z : at_z + 1, :]
-        copies = halo_copies(window)
-        for copy, sends, receives in copies[:2]:
-            @pl.when(sends)
+    messages = (
+        (in_yu, {"dev": 1}), (in_yd, {"dev": -1}), (in_zu, {"gz": 1}), (in_zd, {"gz": -1}),
+        (in_zy, {"gz": -1, "dev": 1}), (in_yz, {"dev": -1, "gz": 1}),
+        (in_xu, {"xy": 1}), (in_xd, {"xy": -1}),
+        (in_yx, {"dev": 1, "xy": -1}), (in_zx, {"gz": 1, "xy": -1}), (in_xz, {"xy": 1, "gz": -1}), (in_xy, {"xy": 1, "dev": -1}),
+    )
+    plain = 6
+
+    def within(move, sign):
+        inside = True
+        for axis, step in move.items():
+            spot = place[axis] + sign * step
+            inside = jnp.logical_and(inside, jnp.logical_and(spot >= 0, spot < count[axis]))
+        return inside
+
+    def first_of(n):
+        return (0, 5) if n == 0 else (5 + 3 * (n - 1), 3)
+
+    def views(n):
+        start, length = first_of(n)
+        planes, pair = pl.ds(start, length), pl.ds(2 * n, 2)
+        low, high = pl.ds(0, 8), pl.ds(size_z - 8, 8)
+        return (
+            (out_yu.at[planes], in_yu.at[planes]), (out_yd.at[pair], in_yd.at[pair]),
+            (out_zu.at[planes], in_zu.at[planes]), (out_zd.at[pair], in_zd.at[pair]),
+            (out_zd.at[2 * n, size_y - 1], in_zy.at[n]), (out_yd.at[2 * n, high], in_yz.at[n]),
+            (out_xu.at[n], in_xu.at[n]), (out_xd.at[n], in_xd.at[n]),
+            (out_xd.at[n], in_yx.at[n]), (out_xd.at[n, high], in_zx.at[n]),
+            (out_xu.at[n, low], in_xz.at[n]), (out_xu.at[n], in_xy.at[n]),
+        )
+
+    def halo_copy(n, number, source, landing):
+        to = {axis: (place[axis] + step + count[axis]) % count[axis] for axis, step in messages[number][1].items()}
+        return pltpu.make_async_remote_copy(
+            src_ref=source,
+            dst_ref=landing,
+            send_sem=halo_send.at[number],
+            recv_sem=halo_got.at[n % 2, number],
+            device_id=to,
+            device_id_type=MESH,
+        )
+
+    def start_halo(n, numbers):
+        for number in numbers:
+            @pl.when(within(messages[number][1], 1))
             def _():
-                copy.start()
+                halo_copy(n, number, *views(n)[number]).start()
+
+    def wait_halo(n):
+        for number in range(len(messages)):
+            @pl.when(within(messages[number][1], -1))
+            def _():
+                halo_copy(n, number, *views(n)[number]).wait_recv()
+
+    def pack(values, high):
         packed = jnp.zeros((size_z, LANES), F32)
-        for k in range(2):
+        for k, value in enumerate(values):
             for y in range(size_y):
                 spot = k * size_y + y
-                amount = spot if ahead else (spot + 1) % LANES
-                value = for_x[k][y]
-                turned = pltpu.roll(value, amount, 1) if amount else value
+                amount = (spot + 1) % LANES if high else spot
+                turned = pltpu.roll(value[y], amount, 1) if amount else value[y]
                 packed = jnp.where(lane == spot, turned, packed)
-        send_x[window] = packed
-        copy, sends, receives = copies[2]
-
-        @pl.when(sends)
+        return packed
+
+    def stage(n, ex, ey, ez, for_y, for_z, for_x):
+        start, _ = first_of(n)
+        for k, value in enumerate((ex, ey, ez) + for_y):
+            out_yu[start + k] = value[size_y - 1]
+        for k, value in enumerate((ez, ex)):
+            out_yd[2 * n + k] = value[0]
+        for k, value in enumerate((ex, ey, ez) + for_z):
+            out_zu[start + k] = value[:, size_z - 1 : size_z, :]
+        for k, value in enumerate((ey, ex)):
+            out_zd[2 * n + k] = value[:, 0:1, :]
+        yield
+        out_xu[n] = pack((ex, ey, ez) + for_x, True)
+        out_xd[n] = pack((ez, ey), False)
+        yield
+
+    for landing, move in messages:
+        @pl.when(jnp.logical_not(within(move, -1)))
         def _():
-            copy.start()
-
-    def wait_halo(window):
-        for copy, sends, receives in halo_copies(window):
-            @pl.when(receives)
-            def _():
-                copy.wait_recv()
+            landing[...] = jnp.zeros(landing.shape, F32)
 
     def inner(ahead, axis, value):
         if axis == 0:
@@ -255,57 +289,105 @@
             return jnp.where(spots == length - 1, 0.0, pltpu.roll(value, length - 1, axis)) - value
         return value - jnp.where(spots == 0, 0.0, pltpu.roll(value, 1, axis))
 
-    def edge_y(window, k):
-        other = got_y[window, k][None]
-        none = jnp.zeros((size_y - 1, size_z, LANES), F32)
-        return jnp.concatenate([none, other] if window % 2 == 0 else [other, none], axis=0)
-
-    def edge_z(window, k):
-        return jnp.where(row3 == (size_z - 1 if window % 2 == 0 else 0), got_z[window, k], 0.0)
-
-    def edge_x(window, k):
-        landed = got_x[window]
+    none = jnp.zeros((size_y - 1, size_z, LANES), F32)
+
+    def at_y(plane, ahead):
+        return jnp.concatenate([none, plane[None]] if ahead else [plane[None], none], axis=0)
+
+    def at_z(rows, ahead):
+        return jnp.where(row3 == (size_z - 1 if ahead else 0), rows, 0.0)
+
+    def at_x(packed, k, ahead):
         edges = []
         for y in range(size_y):
             spot = k * size_y + y
-            amount = (LANES - 1 - spot) if window % 2 == 0 else (LANES - spot) % LANES
-            edges.append(pltpu.roll(landed, amount, 1) if amount else landed)
-        return jnp.where(lane3 == (size_x - 1 if window % 2 == 0 else 0), jnp.stack(edges, axis=0), 0.0)
-
+            amount = (LANES - 1 - spot) if ahead else (LANES - spot) % LANES
+            edges.append(pltpu.roll(packed, amount, 1) if amount else packed)
+        return jnp.where(lane3 == (size_x - 1 if ahead else 0), jnp.stack(edges, axis=0), 0.0)
+
+    def turn(value, by, axis):
+        return pltpu.roll(value, by % value.shape[axis], axis)
+
+    row2 = iota((size_z, LANES), 0)
+    lane_row = iota((size_y, 1, LANES), 2)
+    half_y = jnp.where(dev > 0, COURANT, 0.0)
+    half_z = jnp.where(gz > 0, COURANT, 0.0)
+    half_x = jnp.where(xy > 0, COURANT, 0.0)
+
+    loading[0].wait()
     ex, ey, ez = fields[0], fields[1], fields[2]
-    start_halo(0, (ez, ex), (ey, ex), (ez, ey))
+    hx, hy, hz = fields[3], fields[4], fields[5]
+    for _ in stage(0, ex, ey, ez, (hx, hz), (hx, hy), (hy, hz)):
+        pass
+    pl.semaphore_wait(barrier, beside)
+    start_halo(0, range(len(messages)))
+    pass_on()
+    for copy in loading[1:3]:
+        copy.wait()
+    geometry()
+    run_s, run_c = sincos((phase[0] + 0.5 * ANGULAR_STEP * (iota((8, LANES), 0).astype(F32) + 1.0)) * (0.5 / math.pi))
     loading[3].wait()
     rate = COURANT / permit[...]
     for copy in loading[4:]:
         copy.wait()
-    hx, hy, hz = fields[3], fields[4], fields[5]
     spec_from = spectra
     for n in range(STEPS):
-        window = 2 * n
         hx = hx - COURANT * (inner(True, 0, ez) - inner(True, 1, ey))
         hy = hy - COURANT * (inner(True, 1, ex) - inner(True, 2, ez))
         hz = hz - COURANT * (inner(True, 2, ey) - inner(True, 0, ex))
-        tables_of(window)
-        wait_halo(window)
-        hx = hx - COURANT * (edge_y(window, 0) - edge_z(window, 0))
-        hy = hy - COURANT * (edge_z(window, 1) - edge_x(window, 0))
-        hz = hz - COURANT * (edge_x(window, 1) - edge_y(window, 1))
-        window = 2 * n + 1
-        start_halo(window, (hz, hx), (hy, hx), (hz, hy))
+        tables_of(n)
+        if n == 1:
+            def relay(k, carry):
+                hear()
+                pass_on()
+                return carry
+
+            lax.fori_loop(0, slabs - 3, relay, 0)
+        wait_halo(n)
+        start, _ = first_of(n)
+        xp = in_xd[n]
+        hx = hx - COURANT * (at_y(in_yd[2 * n], True) - at_z(in_zd[2 * n], True))
+        hy = hy - COURANT * (at_z(in_zd[2 * n + 1], True) - at_x(xp, 0, True))
+        hz = hz - COURANT * (at_x(xp, 1, True) - at_y(in_yd[2 * n + 1], True))
+
+        ax, ay, az = in_yu[start], in_yu[start + 1], in_yu[start + 2]
+        bx, by, bz = in_zu[start], in_zu[start + 1], in_zu[start + 2]
+        c_ex, own = in_xu[n], out_xd[n]
+        if n == 0:
+            y_hx, y_hz = in_yu[3], in_yu[4]
+            z_hx, z_hy = in_zu[3], in_zu[4]
+            x_hy, x_hz = turn(c_ex, -3 * size_y, 1), turn(c_ex, -4 * size_y, 1)
+        ay_z = jnp.where(row2 == size_z - 1, in_zy[n], turn(ay, -1, 0))
+        ay_x = jnp.where(lane == size_x - 1, turn(in_yx[n], -2 * size_y, 1), turn(ay, -1, 1))
+        y_hx = y_hx - half_y * ((ez[0] - az) - (ay_z - ay))
+        y_hz = y_hz - half_y * ((ay_x - ay) - (ex[0] - ax))
+        bz_y = jnp.concatenate([bz[1:], in_yz[n, 7:8, :][None]], axis=0)
+        corner = in_zx[n, 7:8, :]
+        bz_x = jnp.stack([turn(corner, -1 - y, 1) for y in range(size_y)], axis=0)
+        bz_x = jnp.where(lane_row == size_x - 1, bz_x, jnp.stack([turn(bz[y], -1, 1) for y in range(size_y)], axis=0))
+        z_hx = z_hx - half_z * ((bz_y - bz) - (ey[:, 0:1, :] - by))
+        z_hy = z_hy - half_z * ((ex[:, 0:1, :] - bx) - (bz_x - bz))
+        c_z = jnp.where(row2 == size_z - 1, in_xz[n, 0:1, :], turn(c_ex, -1, 0))
+        c_y = jnp.where(lane == size_y - 1, turn(in_xy[n], size_y - 1, 1), turn(c_ex, -1, 1))
+        x_hy = x_hy - half_x * ((c_z - c_ex) - (own - turn(c_ex, -2 * size_y, 1)))
+        x_hz = x_hz - half_x * ((turn(own, -size_y, 1) - turn(c_ex, -size_y, 1)) - (c_y - c_ex))
+
+        ex = ex + rate * (inner(False, 0, hz) - inner(False, 1, hy))
+        ey = ey + rate * (inner(False, 1, hx) - inner(False, 2, hz))
+        ez = ez + rate * (inner(False, 2, hy) - inner(False, 0, hx))
+        ex = ex - rate * (at_y(y_hz, False) - at_z(z_hy, False))
+        ey = ey - rate * (at_z(z_hx, False) - at_x(x_hz, 0, False))
+        ez = ez - rate * (at_x(x_hy, 0, False) - at_y(y_hx, False))
+        if n < STEPS - 1:
+            staging = stage(n + 1, ex, ey, ez, (), (), ())
+            next(staging)
+            start_halo(n + 1, range(plain))
+            next(staging)
+            start_halo(n + 1, range(plain, len(messages)))
         half_c, half_s = run_c[2 * n : 2 * n + 1, :], run_s[2 * n : 2 * n + 1, :]
         for c, value in enumerate((hx, hy, hz)):
             spectra_out[3 + c] = spec_from[3 + c] + value * half_c
             spectra_out[9 + c] = spec_from[9 + c] - value * half_s
-        ex = ex + rate * (inner(False, 0, hz) - inner(False, 1, hy))
-        ey = ey + rate * (inner(False, 1, hx) - inner(False, 2, hz))
-        ez = ez + rate * (inner(False, 2, hy) - inner(False, 0, hx))
-        tables_of(window)
-        wait_halo(window)
-        ex = ex - rate * (edge_y(window, 0) - edge_z(window, 0))
-        ey = ey - rate * (edge_z(window, 1) - edge_x(window, 0))
-        ez = ez - rate * (edge_x(window, 1) - edge_y(window, 1))
-        if n < STEPS - 1:
-            start_halo(window + 1, (ez, ex), (ey, ex), (ez, ey))
         full_c, full_s = run_c[2 * n + 1 : 2 * n + 2, :], run_s[2 * n + 1 : 2 * n + 2, :]
         for c, value in enumerate((ex, ey, ez)):
             spectra_out[c] = spec_from[c] + value * full_c
@@ -350,27 +432,22 @@
         owner_row = jnp.where(lanes8 == 8 * gz + p, (wall_owner[0, p] + 1).astype(F32), owner_row)
     own_walls[pl.ds(size_y, 1), :] = owner_row
 
-    def wall_copy(k):
+    def wall_copy(k, ref=None):
+        held = walls.at[gz] if ref is None else ref
         return pltpu.make_async_remote_copy(
-            src_ref=walls.at[gz],
-            dst_ref=walls.at[gz],
-            send_sem=wall_send.at[k],
-            recv_sem=wall_got.at[gz],
+            src_ref=held,
+            dst_ref=held,
+            send_sem=wall_send,
+            recv_sem=wall_got,
             device_id={"gz": (gz + k) % slabs},
             device_id_type=MESH,
-        )
-
-    def wall_landing(s):
-        return pltpu.make_async_remote_copy(
-            src_ref=walls.at[s], dst_ref=walls.at[s], send_sem=wall_send.at[0], recv_sem=wall_got.at[s],
-            device_id={"gz": (gz + 1) % slabs}, device_id_type=MESH,
         )
 
     def cap_copy(k, at):
         return pltpu.make_async_remote_copy(
             src_ref=caps.at[at],
             dst_ref=caps.at[at],
-            send_sem=cap_send.at[k],
+            send_sem=cap_send.at[k - 1],
             recv_sem=cap_got.at[at],
             device_id={"gz": (gz + k) % slabs},
             device_id_type=MESH,
@@ -424,8 +501,8 @@
         return pltpu.make_async_remote_copy(
             src_ref=parts_out.at[pl.ds(owner * per, per)],
             dst_ref=parts_in.at[source],
-            send_sem=part_send.at[owner],
-            recv_sem=part_got.at[source],
+            send_sem=part_send,
+            recv_sem=part_got,
             device_id=ident(flat_of(owner)),
             device_id_type=MESH,
         )
@@ -445,6 +522,7 @@
 
         return carry
 
+    hear()
     lax.fori_loop(0, owners // together, far_and_send, 0)
 
     for k in range(1, slabs):
@@ -464,20 +542,24 @@
 
         lax.fori_loop(1, peers, body, 0)
 
-    def total_copy(k, owner):
+    def total_copy(k, owner, ref=None):
+        held = totals.at[pl.ds(owner * per, per)] if ref is None else ref
         return pltpu.make_async_remote_copy(
-            src_ref=totals.at[pl.ds(owner * per, per)],
-            dst_ref=totals.at[pl.ds(owner * per, per)],
-            send_sem=total_send.at[k],
-            recv_sem=total_got.at[owner],
+            src_ref=held,
+            dst_ref=held,
+            send_sem=total_send,
+            recv_sem=total_got.at[owner // together],
             device_id=ident((me + k) % peers),
             device_id_type=MESH,
         )
 
     @pl.when(leads)
     def _():
+        everyone = parts_in.at[pl.ds(0, peers - 1)]
+        pltpu.make_async_remote_copy(
+            src_ref=everyone, dst_ref=everyone, send_sem=part_send, recv_sem=part_got, device_id={"gz": gz}, device_id_type=MESH
+        ).wait_recv()
         parts_in[me] = parts_out[pl.ds(mine * per, per)]
-        each_peer(lambda k: part_copy(0, (me + k) % peers).wait_recv())
         totals[pl.ds(mine * per, per)] = jnp.sum(parts_in[...], axis=0)
         each_peer(lambda k: total_copy(peers - k, mine).start())
 
@@ -491,10 +573,7 @@
         return jnp.dot(chooser, records, precision=HIGHEST, preferred_element_type=F32)[:share]
 
     def choose_owned():
-        for s in range(slabs):
-            @pl.when(s != gz)
-            def _():
-                wall_landing(s).wait_recv()
+        wall_copy(1, walls.at[pl.ds(0, slabs - 1)]).wait_recv()
         for at, holder in enumerate((0, slabs - 1)):
             @pl.when(gz != holder)
             def _():
@@ -540,10 +619,17 @@
 
     def adjoint_some(number, total):
         several = [partner(together * number + m) for m in range(together)]
-        for owner in several:
-            @pl.when(owner != mine)
+        batch = several[0] // together
+        ours = jnp.logical_and(leads, mine // together == batch)
+
+        @pl.when(jnp.logical_not(ours))
+        def _():
+            total_copy(1, several[0], totals.at[pl.ds(batch * bunch, bunch)]).wait_recv()
+
+        if together > 1:
+            @pl.when(ours)
             def _():
-                total_copy(1, owner).wait_recv()
+                total_copy(1, several[0], totals.at[pl.ds(batch * bunch, bunch - per)]).wait_recv()
 
         for owner in several:
             for m in range(per):
@@ -561,31 +647,31 @@
         cap = block_transpose(gradient[8 * y : 8 * y + 8, :size_x] * (norm * end_weight))
         adjoint_out[pl.ds(size_y + 8 * y, 8), 0, :] = cap
 
-    for window in range(windows):
-        for copy, sends, receives in halo_copies(window):
-            @pl.when(sends)
-            def _():
-                copy.wait_send()
-
-    def part_sent(owner, carry):
-        @pl.when(owner != mine)
+    for number, (landing, move) in enumerate(messages):
+        @pl.when(within(move, 1))
         def _():
-            part_copy(owner, me).wait_send()
-
-        return carry
-
-    lax.fori_loop(0, owners, part_sent, 0)
-    for k in range(1, slabs):
-        wall_copy(k).wait_send()
+            halo_copy(0, number, landing, landing).wait_send()
+
+    def parts_sent(ref):
+        pltpu.make_async_remote_copy(
+            src_ref=ref, dst_ref=ref, send_sem=part_send, recv_sem=part_got, device_id={"gz": gz}, device_id_type=MESH
+        ).wait_send()
+
+    @pl.when(leads)
+    def _():
+        parts_sent(parts_out.at[pl.ds(0, (owners - 1) * per)])
+        total_copy(1, 0, parts_in.at[pl.ds(0, peers - 1)]).wait_send()
+
+    @pl.when(jnp.logical_not(leads))
+    def _():
+        parts_sent(parts_out)
+
+    wall_copy(1, walls.at[pl.ds(0, slabs - 1)]).wait_send()
     for at, holder in enumerate((0, slabs - 1)):
         @pl.when(gz == holder)
         def _():
             for k in range(1, slabs):
                 cap_copy(k, at).wait_send()
-
-    @pl.when(leads)
-    def _():
-        each_peer(lambda k: total_copy(k, mine).wait_send())
 
 
 def write_out(*refs):
@@ -611,7 +697,12 @@
     owned = size_y + 2 * (cap_count // slabs)
     rows = 16 * size_y
     depth = size_x + 8 * size_z
-    windows = 2 * STEPS
+    planes, pairs = 5 + 3 * (STEPS - 1), 2 * STEPS
+    halos = (
+        (planes, size_z, LANES), (pairs, size_z, LANES), (planes, size_y, 1, LANES), (pairs, size_y, 1, LANES),
+        (STEPS, size_z, LANES), (STEPS, size_z, LANES),
+        (STEPS, 1, LANES), (STEPS, 8, LANES), (STEPS, size_z, LANES), (STEPS, 8, LANES), (STEPS, 8, LANES), (STEPS, size_z, LANES),
+    )
     vmem = pl.BlockSpec(memory_space=pltpu.VMEM)
     anywhere = pl.BlockSpec(memory_space=pl.ANY)
     dma = pltpu.SemaphoreType.DMA
@@ -627,12 +718,8 @@
         in_specs=[anywhere] * 9,
         out_specs=(vmem,) * 5,
         scratch_shapes=[
-            pltpu.VMEM((windows, 2, size_z, LANES), F32),
-            pltpu.VMEM((windows, 2, size_y, 1, LANES), F32),
-            pltpu.VMEM((windows, size_z, LANES), F32),
-            pltpu.VMEM((windows, 2, size_z, LANES), F32),
-            pltpu.VMEM((windows, 2, size_y, 1, LANES), F32),
-            pltpu.VMEM((windows, size_z, LANES), F32),
+            *(pltpu.VMEM(shape, F32) for shape in halos[:6]),
+            *(pltpu.VMEM(shape, F32) for shape in halos),
             pltpu.VMEM(fields.shape, F32),
             pltpu.VMEM(spectra.shape, F32),
             pltpu.VMEM(permittivity.shape, F32),
@@ -654,12 +741,12 @@
             pltpu.VMEM((chunks, 4, LANES), F32),
             pltpu.VMEM((slabs, 8, LANES), F32),
             pltpu.VMEM((2, cap_count, LANES), F32),
-            dma((windows, 3)), dma((windows, 3)),
-            dma((owners,)), dma((peers,)),
-            dma((peers,)), dma((owners,)),
-            dma((slabs,)), dma((slabs,)),
-            dma((slabs,)), dma((2,)),
-            dma((9,)),
+            dma((len(halos),)), dma((2, len(halos))),
+            dma, dma,
+            dma, dma((owners // max(1, 4 // per),)),
+            dma, dma,
+            dma((slabs - 1,)), dma((2,)),
+            dma((9,)), pltpu.SemaphoreType.REGULAR((2,)),
         ],
         compiler_params=pltpu.CompilerParams(collective_id=0, has_side_effects=True),
     )(

time: 35.5 us -> 27.2 us (0.77)
  Pallas kernels: 34 us -> 25.7 us
    pallas_call x1, Pallas kernels: 33.2 us -> 24.9 us  [local(): pl.pallas_call(functools.partial(kernel, (slabs, devs, xys)), out_shape=(...]
where the time goes in v2:
time: 27.2 us; the launch traced here: 27 us
  Pallas kernels  25.7 us (94%)
  between operations  1.29 us (5%)
    pallas_call x1, Pallas kernels, local(): pl.pallas_call(functools.partial(kernel, (slabs, devs, xys)), out_shape=(...  24.9 us
    pallas_call x1, Pallas kernels, local(): pl.pallas_call(write_out, out_shape=tuple((jax.ShapeDtypeStruct(shape, F3...  0.86 us

profile of v2, /device:TPU:0, one launch (start us, length us, event | category | flops | bytes accessed | tf_op | source)
XLA Modules:
  0.0 27.0 jit_solution(16453290166352723853)
XLA Ops:
  1.3 24.9 %shard_map.128 = (f32[6,4,16,128]{3,2,1,0:T(8,128)S(1)}, f32[12,4,16,128]{3,2,1,0:T(8,128)S(1)}, f32[20,1,128]{2,1,0:T(1,128)S(1)}, f32[1,128]{1,0:T(1,128)S(1)}, f32[36,1,128]{2,1,0:T(1,128)S(1)}) custom-call(f32[6,4,16,128]{3,2,1,0:T(8,128)} %fields_in.1, f32[12,4,16,128]{3,2,1,0:T(8,128)} %spectra_in.1, f32[4,16,128]{2,1,0:T(8,128)} %permit_in.1, ...), custom_call_target="tpu_custom_call" | custom-call | tf_op jit(solution)/shard_map/pallas_call | solution.py:709
  26.2 0.9 %shard_map.129 = (f32[6,4,16,128]{3,2,1,0:T(8,128)}, f32[12,4,16,128]{3,2,1,0:T(8,128)}, f32[20,1,128]{2,1,0:T(1,128)}, f32[1,128]{1,0:T(1,128)}, f32[36,1,128]{2,1,0:T(1,128)}) custom-call(f32[6,4,16,128]{3,2,1,0:T(8,128)S(1)} %get-tuple-element.15.refs_0_, f32[12,4,16,128]{3,2,1,0:T(8,128)S(1)} %get-tuple-element.16.refs_1_, ...), custom_call_target="tpu_custom_call" | custom-call | tf_op jit(solution)/shard_map/pallas_call | solution.py:757

commit v3 on v2

--- a/solution.py
+++ b/solution.py
@@ -44,6 +44,11 @@
     return high, (values - high.astype(F32)).astype(BF16)
 
 
+def arrival_rows(n, size_y, size_z):
+    length = 5 if n == 0 else 3
+    return (length + 2) * (size_z + size_y) + 1 + 3 * 8 + 4 * size_z
+
+
 def block_transpose(tile):
     on_diagonal = (iota(tile.shape, 1) // PATCH) == iota(tile.shape, 0)
     total = jnp.where(on_diagonal, tile, 0.0)
@@ -58,7 +63,7 @@
     fields_in, spectra_in, permit_in, phase_in, wall_owner_in, cap_owner_in, dirs_in, target_in, aim_in,
     fields_out, spectra_out, owned_out, intensity_out, adjoint_out,
     out_yu, out_yd, out_zu, out_zd, out_xu, out_xd,
-    in_yu, in_yd, in_zu, in_zd, in_xu, in_xd, in_zy, in_yz, in_yx, in_zx, in_xz, in_xy,
+    in_yu, in_yd, in_zu, in_zd, in_xu, in_xd, in_zy, in_yz, in_yx, in_zx, in_xz, in_xy, blank, blank_rows, arrivals,
     fields, spectra, permit, phase, wall_owner, cap_owner, dirs, target, aim,
     geo, weights, phases, table_hi, table_lo, cap_plane, lhs,
     parts_out, parts_in, totals, walls, caps,
@@ -83,6 +88,7 @@
     def ident(flat):
         return {"gz": flat // (devs * xys), "dev": (flat // xys) % devs, "xy": flat % xys}
 
+    pltpu.make_async_copy(fields_in, fields, loads.at[0]).start()
     barrier = pltpu.get_barrier_semaphore()
 
     for away in (1, -1, 0):
@@ -118,7 +124,7 @@
             (wall_owner_in, wall_owner), (cap_owner_in, cap_owner), (target_in, target), (aim_in, aim),
         ))
     ]
-    for copy in loading:
+    for copy in loading[1:]:
         copy.start()
 
     def geometry():
@@ -199,7 +205,6 @@
         (in_xu, {"xy": 1}), (in_xd, {"xy": -1}),
         (in_yx, {"dev": 1, "xy": -1}), (in_zx, {"gz": 1, "xy": -1}), (in_xz, {"xy": 1, "gz": -1}), (in_xy, {"xy": 1, "dev": -1}),
     )
-    plain = 6
 
     def within(move, sign):
         inside = True
@@ -230,7 +235,7 @@
             src_ref=source,
             dst_ref=landing,
             send_sem=halo_send.at[number],
-            recv_sem=halo_got.at[n % 2, number],
+            recv_sem=halo_got.at[n],
             device_id=to,
             device_id_type=MESH,
         )
@@ -241,11 +246,19 @@
             def _():
                 halo_copy(n, number, *views(n)[number]).start()
 
+    def fill_halo(n):
+        length = first_of(n)[1]
+        planes, pair, rows, row_pair = blank.at[pl.ds(0, length)], blank.at[pl.ds(0, 2)], blank_rows.at[pl.ds(0, length)], blank_rows.at[pl.ds(0, 2)]
+        plane, tile = blank.at[0], blank.at[0, pl.ds(0, 8)]
+        sources = (planes, pair, rows, row_pair, blank_rows.at[0, 0], tile, plane, plane, plane, tile, tile, plane)
+        for number, source in enumerate(sources):
+            @pl.when(jnp.logical_not(within(messages[number][1], -1)))
+            def _():
+                pltpu.make_async_copy(source, views(n)[number][1], halo_got.at[n]).start()
+
     def wait_halo(n):
-        for number in range(len(messages)):
-            @pl.when(within(messages[number][1], -1))
-            def _():
-                halo_copy(n, number, *views(n)[number]).wait_recv()
+        everything = arrivals.at[pl.ds(0, arrival_rows(n, size_y, size_z))]
+        pltpu.make_async_copy(everything, everything, halo_got.at[n]).wait()
 
     def pack(values, high):
         packed = jnp.zeros((size_z, LANES), F32)
@@ -272,10 +285,8 @@
         out_xd[n] = pack((ez, ey), False)
         yield
 
-    for landing, move in messages:
-        @pl.when(jnp.logical_not(within(move, -1)))
-        def _():
-            landing[...] = jnp.zeros(landing.shape, F32)
+    blank[...] = jnp.zeros(blank.shape, F32)
+    blank_rows[...] = jnp.zeros(blank_rows.shape, F32)
 
     def inner(ahead, axis, value):
         if axis == 0:
@@ -320,12 +331,15 @@
     for _ in stage(0, ex, ey, ez, (hx, hz), (hx, hy), (hy, hz)):
         pass
     pl.semaphore_wait(barrier, beside)
-    start_halo(0, range(len(messages)))
+    start_halo(0, (4, 5, 8, 11, 9, 10, 0, 1, 2, 3, 6, 7))
+    fill_halo(0)
     pass_on()
     for copy in loading[1:3]:
         copy.wait()
     geometry()
     run_s, run_c = sincos((phase[0] + 0.5 * ANGULAR_STEP * (iota((8, LANES), 0).astype(F32) + 1.0)) * (0.5 / math.pi))
+    for n in range(1, STEPS):
+        fill_halo(n)
     loading[3].wait()
     rate = COURANT / permit[...]
     for copy in loading[4:]:
@@ -381,9 +395,9 @@
         if n < STEPS - 1:
             staging = stage(n + 1, ex, ey, ez, (), (), ())
             next(staging)
-            start_halo(n + 1, range(plain))
+            start_halo(n + 1, (4, 5, 0, 1, 2, 3))
             next(staging)
-            start_halo(n + 1, range(plain, len(messages)))
+            start_halo(n + 1, (8, 11, 9, 10, 6, 7))
         half_c, half_s = run_c[2 * n : 2 * n + 1, :], run_s[2 * n : 2 * n + 1, :]
         for c, value in enumerate((hx, hy, hz)):
             spectra_out[3 + c] = spec_from[3 + c] + value * half_c
@@ -447,7 +461,7 @@
         return pltpu.make_async_remote_copy(
             src_ref=caps.at[at],
             dst_ref=caps.at[at],
-            send_sem=cap_send.at[k - 1],
+            send_sem=cap_send,
             recv_sem=cap_got.at[at],
             device_id={"gz": (gz + k) % slabs},
             device_id_type=MESH,
@@ -535,13 +549,6 @@
             for k in range(1, slabs):
                 cap_copy(k, at).start()
 
-    def each_peer(act):
-        def body(k, carry):
-            act(k)
-            return carry
-
-        lax.fori_loop(1, peers, body, 0)
-
     def total_copy(k, owner, ref=None):
         held = totals.at[pl.ds(owner * per, per)] if ref is None else ref
         return pltpu.make_async_remote_copy(
@@ -561,7 +568,20 @@
         ).wait_recv()
         parts_in[me] = parts_out[pl.ds(mine * per, per)]
         totals[pl.ds(mine * per, per)] = jnp.sum(parts_in[...], axis=0)
-        each_peer(lambda k: total_copy(peers - k, mine).start())
+        for k in sorted(range(slabs), key=lambda k: -min(k, slabs - k)):
+            row = (gz + k) % slabs * across
+
+            def send(r, carry):
+                to = row + (dev * xys + xy + r) % across
+
+                @pl.when(to != me)
+                def _():
+                    total_copy((to - me + peers) % peers, mine).start()
+
+                return carry
+
+            lax.fori_loop(0, across, send, 0, unroll=across <= 4)
+
 
     def choose(mine, share, records):
         length = mine.shape[1]
@@ -637,9 +657,8 @@
         return total
 
     rounds = owners // together
-    gradient = lax.fori_loop(0, rounds // 2, adjoint_some, jnp.zeros((all_rows, size_x + 8 * size_z), F32))
     choose_owned()
-    gradient = lax.fori_loop(rounds // 2, rounds, adjoint_some, gradient)
+    gradient = lax.fori_loop(0, rounds, adjoint_some, jnp.zeros((all_rows, size_x + 8 * size_z), F32))
     intensity_out[...] = intensity_of(totals[me // ratio])
     for y in range(size_y):
         wall = gradient[half_rows + 8 * y : half_rows + 8 * y + 8, size_x:]
@@ -670,8 +689,8 @@
     for at, holder in enumerate((0, slabs - 1)):
         @pl.when(gz == holder)
         def _():
-            for k in range(1, slabs):
-                cap_copy(k, at).wait_send()
+            sent = weights.at[pl.ds(0, slabs - 1)]
+            pltpu.make_async_copy(sent, sent, cap_send).wait()
 
 
 def write_out(*refs):
@@ -720,6 +739,9 @@
         scratch_shapes=[
             *(pltpu.VMEM(shape, F32) for shape in halos[:6]),
             *(pltpu.VMEM(shape, F32) for shape in halos),
+            pltpu.VMEM((5, size_z, LANES), F32),
+            pltpu.VMEM((5, size_y, 1, LANES), F32),
+            pltpu.VMEM((arrival_rows(0, size_y, size_z), 1, LANES), F32),
             pltpu.VMEM(fields.shape, F32),
             pltpu.VMEM(spectra.shape, F32),
             pltpu.VMEM(permittivity.shape, F32),
@@ -741,11 +763,11 @@
             pltpu.VMEM((chunks, 4, LANES), F32),
             pltpu.VMEM((slabs, 8, LANES), F32),
             pltpu.VMEM((2, cap_count, LANES), F32),
-            dma((len(halos),)), dma((2, len(halos))),
+            dma((len(halos),)), dma((STEPS,)),
             dma, dma,
             dma, dma((owners // max(1, 4 // per),)),
             dma, dma,
-            dma((slabs - 1,)), dma((2,)),
+            dma, dma((2,)),
             dma((9,)), pltpu.SemaphoreType.REGULAR((2,)),
         ],
         compiler_params=pltpu.CompilerParams(collective_id=0, has_side_effects=True),

time: 27.2 us -> 26.4 us (0.971)
  Pallas kernels: 25.7 us -> 25 us
    pallas_call x1, Pallas kernels: 24.9 us -> 24.1 us  [local(): pl.pallas_call(functools.partial(kernel, (slabs, devs, xys)), out_shape=(...]
where the time goes in v3:
time: 26.4 us; the launch traced here: 26.3 us
  Pallas kernels  25 us (95%)
  between operations  1.29 us (5%)
    pallas_call x1, Pallas kernels, local(): pl.pallas_call(functools.partial(kernel, (slabs, devs, xys)), out_shape=(...  24.1 us
    pallas_call x1, Pallas kernels, local(): pl.pallas_call(write_out, out_shape=tuple((jax.ShapeDtypeStruct(shape, F3...  0.86 us

profile of v3, /device:TPU:0, one launch (start us, length us, event | category | flops | bytes accessed | tf_op | source)
XLA Modules:
  0.0 26.3 jit_solution(1976139627017485003)
XLA Ops:
  1.3 24.1 %shard_map.128 = (f32[6,4,16,128]{3,2,1,0:T(8,128)S(1)}, f32[12,4,16,128]{3,2,1,0:T(8,128)S(1)}, f32[20,1,128]{2,1,0:T(1,128)S(1)}, f32[1,128]{1,0:T(1,128)S(1)}, f32[36,1,128]{2,1,0:T(1,128)S(1)}) custom-call(f32[6,4,16,128]{3,2,1,0:T(8,128)} %fields_in.1, f32[12,4,16,128]{3,2,1,0:T(8,128)} %spectra_in.1, f32[4,16,128]{2,1,0:T(8,128)} %permit_in.1, ...), custom_call_target="tpu_custom_call" | custom-call | tf_op jit(solution)/shard_map/pallas_call | solution.py:728
  25.4 0.9 %shard_map.129 = (f32[6,4,16,128]{3,2,1,0:T(8,128)}, f32[12,4,16,128]{3,2,1,0:T(8,128)}, f32[20,1,128]{2,1,0:T(1,128)}, f32[1,128]{1,0:T(1,128)}, f32[36,1,128]{2,1,0:T(1,128)}) custom-call(f32[6,4,16,128]{3,2,1,0:T(8,128)S(1)} %get-tuple-element.15.refs_0_, f32[12,4,16,128]{3,2,1,0:T(8,128)S(1)} %get-tuple-element.16.refs_1_, ...), custom_call_target="tpu_custom_call" | custom-call | tf_op jit(solution)/shard_map/pallas_call | solution.py:779

commit v4 on v3

--- a/solution.py
+++ b/solution.py
@@ -64,10 +64,11 @@
     fields_out, spectra_out, owned_out, intensity_out, adjoint_out,
     out_yu, out_yd, out_zu, out_zd, out_xu, out_xd,
     in_yu, in_yd, in_zu, in_zd, in_xu, in_xd, in_zy, in_yz, in_yx, in_zx, in_xz, in_xy, blank, blank_rows, arrivals,
+    out_w, out_x, land_w, land_x, cap_e, cap_h, cap_r, empty, cap_sum,
     fields, spectra, permit, phase, wall_owner, cap_owner, dirs, target, aim,
     geo, weights, phases, table_hi, table_lo, cap_plane, lhs,
     parts_out, parts_in, totals, walls, caps,
-    halo_send, halo_got, part_send, part_got, total_send, total_got, wall_send, wall_got, cap_send, cap_got, loads, chain,
+    halo_send, halo_got, part_send, part_got, total_send, total_got, wall_send, wall_got, cap_send, cap_got, loads, chain, region_send, region_got,
 ):
     slabs, devs, xys = sizes
     peers = slabs * devs * xys
@@ -325,38 +326,248 @@
     half_z = jnp.where(gz > 0, COURANT, 0.0)
     half_x = jnp.where(xy > 0, COURANT, 0.0)
 
+    zt = pl.multiple_of(jnp.where(gz == 0, 0, size_z - 8), 8)
+    depth = STEPS
+    extent = size_y + 2 * depth
+    quarter = 8 * size_y
+    low_tile, high_tile = pl.ds(0, 8), pl.ds(size_z - 8, 8)
+
+    regions = []
+    for a in (1, -1, 0):
+        for b in (1, -1, 0):
+            if a or b:
+                source = out_w if b == 0 else out_w.at[:, high_tile if b > 0 else low_tile]
+                rows = pl.ds(8, size_z) if b == 0 else pl.ds(0 if b > 0 else size_z + 8, 8)
+                landing = land_w.at[1 - a, :, rows]
+                nothing = blank.at[pl.ds(0, 2)] if b == 0 else empty.at[0, pl.ds(0, 2)]
+                regions.append((0, {"dev": a, "gz": b}, source, landing, landing, nothing))
+    for a in (1, -1, 0):
+        for flip in (0, 1):
+            if a or flip:
+                to = {"dev": a, "flip": flip}
+                regions.append((1, to, out_x, land_x.at[1 - a, xy], land_x.at[1 - a, (xy + flip) % 2], empty.at[0, pl.ds(0, 2)]))
+    for at, a in enumerate((1, -1)):
+        three = pl.ds(size_y - depth, depth) if a > 0 else pl.ds(0, depth)
+        two = pl.ds(size_y - 2, 2) if a > 0 else pl.ds(0, 2)
+        h_planes = three if a > 0 else two
+        h_landing = cap_h.at[at] if a > 0 else cap_h.at[at, :, two]
+        tile = pl.ds(zt, 8)
+        for source, landing, nothing in (
+            (fields_in.at[pl.ds(0, 3), three, tile], cap_e.at[at], empty),
+            (fields_in.at[pl.ds(3, 3), h_planes, tile], h_landing, empty if a > 0 else empty.at[:, two]),
+            (permit_in.at[two, tile], cap_r.at[at], empty.at[0, pl.ds(0, 2)]),
+        ):
+            regions.append((2, {"dev": a}, source, landing, landing, nothing))
+
+    def region_inside(move, sign):
+        return within({axis: step for axis, step in move.items() if axis != "flip" and step}, sign)
+
+    def region_copy(number):
+        kind, move, source, landing, _, _ = regions[number]
+        to = {axis: (place[axis] + step + count[axis]) % count[axis] for axis, step in move.items() if axis != "flip"}
+        if move.get("flip"):
+            to["xy"] = (xy + 1) % 2
+        return pltpu.make_async_remote_copy(
+            src_ref=source,
+            dst_ref=landing,
+            send_sem=region_send.at[number],
+            recv_sem=region_got.at[min(kind, 1)],
+            device_id=to,
+            device_id_type=MESH,
+        )
+
+    def region_when(number, sign):
+        inside = region_inside(regions[number][1], sign)
+        return jnp.logical_and(inside, is_end) if regions[number][0] else inside
+
+    def start_regions(kinds):
+        for number, region in enumerate(regions):
+            if region[0] in kinds:
+                @pl.when(region_when(number, 1))
+                def _():
+                    region_copy(number).start()
+
+    def fill_regions():
+        for number, (kind, move, _, _, landing, nothing) in enumerate(regions):
+            missing = jnp.logical_not(region_inside(move, -1))
+
+            @pl.when(jnp.logical_and(missing, is_end) if kind else missing)
+            def _():
+                pltpu.make_async_copy(nothing, landing, region_got.at[min(kind, 1)]).start()
+
+    def wait_region(which):
+        length = (10 * size_z) if which == 0 else 80 + 296
+        everything = arrivals.at[pl.ds(0, length)]
+        pltpu.make_async_copy(everything, everything, region_got.at[which]).wait()
+
+    def window(slots, amount_of):
+        rows = slots[0].shape[1]
+        spot = iota((rows, LANES), 1)
+        packs = []
+        for part in range(2):
+            packed = jnp.full((rows, LANES), COURANT, F32)
+            for c in range(4 * part, min(4 * part + 4, len(slots))):
+                for y in range(size_y):
+                    base = quarter * (c % 4) + 8 * y
+                    turned = pltpu.roll(slots[c][y], amount_of(base), 1)
+                    packed = jnp.where(jnp.logical_and(spot >= base, spot < base + 8), turned, packed)
+            packs.append(packed)
+        return packs
+
+    empty[...] = jnp.zeros(empty.shape, F32)
+    pl.semaphore_wait(barrier, beside)
+    start_regions((2,))
+    pass_on()
     loading[0].wait()
-    ex, ey, ez = fields[0], fields[1], fields[2]
-    hx, hy, hz = fields[3], fields[4], fields[5]
-    for _ in stage(0, ex, ey, ez, (hx, hz), (hx, hy), (hy, hz)):
+    loading[3].wait()
+    permit[...] = COURANT / permit[...]
+    own = window([fields[c] for c in range(6)] + [permit[...]], lambda base: (base - (x_wall - 4) + 2 * LANES) % LANES)
+    for part in range(2):
+        out_w[part] = own[part]
+        land_w[1, part, pl.ds(8, size_z), :] = own[part]
+
+    @pl.when(is_end)
+    def _():
+        tile = pl.ds(zt, 8)
+        packs = window([fields[c, :, tile, :] for c in range(6)] + [permit[:, tile, :]], lambda base: (base + 4) % LANES)
+        left = iota((8, LANES), 1) % 8 < 4
+        mine_half = jnp.where(xy == 0, 1.0, 0.0)
+        for part in range(2):
+            kept = packs[part] * jnp.where(left, mine_half, 1.0 - mine_half)
+            out_x[part] = kept
+            land_x[1, xy, part] = kept
+
+    @pl.when(jnp.logical_not(is_end))
+    def _():
+        land_x[...] = jnp.zeros(land_x.shape, F32)
+
+    start_regions((1, 0))
+    for _ in stage(0, *(fields[c] for c in range(3)), (fields[3], fields[5]), (fields[3], fields[4]), (fields[4], fields[5])):
         pass
-    pl.semaphore_wait(barrier, beside)
     start_halo(0, (4, 5, 8, 11, 9, 10, 0, 1, 2, 3, 6, 7))
-    fill_halo(0)
-    pass_on()
+    fill_regions()
+    for n in range(STEPS):
+        fill_halo(n)
     for copy in loading[1:3]:
         copy.wait()
     geometry()
     run_s, run_c = sincos((phase[0] + 0.5 * ANGULAR_STEP * (iota((8, LANES), 0).astype(F32) + 1.0)) * (0.5 / math.pi))
-    for n in range(1, STEPS):
-        fill_halo(n)
-    loading[3].wait()
-    rate = COURANT / permit[...]
+    for n in range(STEPS):
+        tables_of(n)
+
+    def relay(k, carry):
+        hear()
+        pass_on()
+        return carry
+
+    lax.fori_loop(0, slabs - 3, relay, 0)
     for copy in loading[4:]:
         copy.wait()
-    spec_from = spectra
+
+    def half_of(n):
+        return run_c[2 * n : 2 * n + 1, :], run_s[2 * n : 2 * n + 1, :]
+
+    def full_of(n):
+        return run_c[2 * n + 1 : 2 * n + 2, :], run_s[2 * n + 1 : 2 * n + 2, :]
+
+    wait_region(0)
+
+    @pl.when(is_end)
+    def _():
+        wait_region(1)
+
+    tall = size_z + 16
+    spot = iota((tall + 8, LANES), 1)
+    joined = [
+        [jnp.concatenate([land_w[dy, part], land_x[dy, 0, part] + land_x[dy, 1, part]], axis=0) for part in range(2)]
+        for dy in range(3)
+    ]
+    held = []
+    for c in range(8):
+        value = jnp.zeros((tall + 8, LANES), F32)
+        first = 0
+        for dy, planes in enumerate((depth, size_y, depth)):
+            start = quarter * (c % 4) + (8 * (size_y - depth) if dy == 0 else 0)
+            chosen = jnp.logical_and(spot >= first, spot < first + 8 * planes)
+            value = jnp.where(chosen, turn(joined[dy][c // 4], first - start, 1), value)
+            first += 8 * planes
+        held.append(value)
+    ex, ey, ez, hx, hy, hz, r, k = held
+    border_e, border_h = [], []
+    sums = [jnp.zeros((size_z, LANES), F32) for _ in range(8)]
     for n in range(STEPS):
+        border_e.append((ez[tall:], ey[tall:]))
+        hx = hx - k * ((turn(ez, -8, 1) - ez) - (turn(ey, -1, 0) - ey))
+        hy = hy - k * ((turn(ex, -1, 0) - ex) - (turn(ez, -1, 1) - ez))
+        hz = hz - k * ((turn(ey, -1, 1) - ey) - (turn(ex, -8, 1) - ex))
+        border_h.append((hz[tall:], hy[tall:]))
+        ex = ex + r * ((hz - turn(hz, 8, 1)) - (hy - turn(hy, 1, 0)))
+        ey = ey + r * ((hx - turn(hx, 1, 0)) - (hz - turn(hz, 1, 1)))
+        ez = ez + r * ((hy - turn(hy, 1, 1)) - (hx - turn(hx, 8, 1)))
+        for at, (value, (co, si)) in enumerate(((hz, half_of(n)), (hy, half_of(n)), (ez, full_of(n)), (ey, full_of(n)))):
+            value = value[8 : 8 + size_z]
+            sums[at] = sums[at] + value * co
+            sums[4 + at] = sums[4 + at] - value * si
+
+    cap_sum[...] = jnp.zeros(cap_sum.shape, F32)
+
+    @pl.when(is_end)
+    def _():
+        tile = pl.ds(zt, 8)
+        eight = iota((8, LANES), 1)
+        left, right = jnp.where(xy == 0, 1.0, 0.0), jnp.where(xy == 0, 0.0, 1.0)
+        behind, ahead = jnp.where(dev > 0, COURANT, 0.0), jnp.where(dev < devs - 1, COURANT, 0.0)
+
+        def rate_of(eps):
+            there = eps > 0.0
+            return jnp.where(there, COURANT / jnp.where(there, eps, 1.0), 0.0)
+
+        e = [[cap_e[0, c, i] for i in range(3)] + [fields[c, y, tile, :] for y in range(size_y)] + [cap_e[1, c, i] for i in range(3)] for c in range(3)]
+        h = [[cap_h[0, c, i] for i in range(3)] + [fields[3 + c, y, tile, :] for y in range(size_y)] + [cap_h[1, c, i] for i in range(2)] for c in range(3)]
+        rates = [None] + [rate_of(cap_r[0, i]) for i in range(2)] + [permit[y, tile, :] for y in range(size_y)] + [rate_of(cap_r[1, i]) for i in range(2)]
+        coefs = [behind] * depth + [COURANT] * size_y + [ahead] * depth
+
+        def next_x(value, border, i):
+            return jnp.where(eight == LANES - 1, turn(border, LANES - 1 - (8 * i + 4), 1), turn(value, -1, 1))
+
+        def last_x(value, border, i):
+            return jnp.where(eight == 0, turn(border, -(8 * i + 3), 1), turn(value, 1, 1))
+
+        totals_of = [[jnp.zeros((8, LANES), F32) for _ in range(8)] for _ in range(size_y)]
+        for n in range(STEPS):
+            bz, by = (value * left for value in border_e[n])
+            fx, fy, fz = [list(v) for v in h]
+            for i in range(n, extent - 1 - n):
+                xs, ys, zs = e[0][i], e[1][i], e[2][i]
+                fx[i] = h[0][i] - coefs[i] * ((e[2][i + 1] - zs) - (turn(ys, -1, 0) - ys))
+                fy[i] = h[1][i] - coefs[i] * ((turn(xs, -1, 0) - xs) - (next_x(zs, bz, i) - zs))
+                fz[i] = h[2][i] - coefs[i] * ((next_x(ys, by, i) - ys) - (e[0][i + 1] - xs))
+            h = [fx, fy, fz]
+            bz, by = (value * right for value in border_h[n])
+            gx, gy, gz_ = [list(v) for v in e]
+            for i in range(n + 1, extent - 1 - n):
+                xs, ys, zs = h[0][i], h[1][i], h[2][i]
+                gx[i] = e[0][i] + rates[i] * ((zs - h[2][i - 1]) - (ys - turn(ys, 1, 0)))
+                gy[i] = e[1][i] + rates[i] * ((xs - turn(xs, 1, 0)) - (zs - last_x(zs, bz, i)))
+                gz_[i] = e[2][i] + rates[i] * ((ys - last_x(ys, by, i)) - (xs - h[0][i - 1]))
+            e = [gx, gy, gz_]
+            for y in range(size_y):
+                i = depth + y
+                for at, (value, (co, si)) in enumerate(((h[1][i], half_of(n)), (h[0][i], half_of(n)), (e[1][i], full_of(n)), (e[0][i], full_of(n)))):
+                    totals_of[y][at] = totals_of[y][at] + value * co
+                    totals_of[y][4 + at] = totals_of[y][4 + at] - value * si
+        for y in range(size_y):
+            for c in range(8):
+                value = totals_of[y][c]
+                cap_sum[pl.ds(8 * y + c, 1), :] = jnp.where(gz == 0, value[ZB : ZB + 1], value[7 - ZB : 8 - ZB])
+
+    def advance(n, ghosts):
+        fields_from, spec_from = (fields, spectra) if n == 0 else (fields_out, spectra_out)
+        ex, ey, ez, hx, hy, hz = (fields_from[c] for c in range(6))
+        rate = permit[...]
         hx = hx - COURANT * (inner(True, 0, ez) - inner(True, 1, ey))
         hy = hy - COURANT * (inner(True, 1, ex) - inner(True, 2, ez))
         hz = hz - COURANT * (inner(True, 2, ey) - inner(True, 0, ex))
-        tables_of(n)
-        if n == 1:
-            def relay(k, carry):
-                hear()
-                pass_on()
-                return carry
-
-            lax.fori_loop(0, slabs - 3, relay, 0)
         wait_halo(n)
         start, _ = first_of(n)
         xp = in_xd[n]
@@ -371,6 +582,8 @@
             y_hx, y_hz = in_yu[3], in_yu[4]
             z_hx, z_hy = in_zu[3], in_zu[4]
             x_hy, x_hz = turn(c_ex, -3 * size_y, 1), turn(c_ex, -4 * size_y, 1)
+        else:
+            y_hx, y_hz, z_hx, z_hy, x_hy, x_hz = ghosts
         ay_z = jnp.where(row2 == size_z - 1, in_zy[n], turn(ay, -1, 0))
         ay_x = jnp.where(lane == size_x - 1, turn(in_yx[n], -2 * size_y, 1), turn(ay, -1, 1))
         y_hx = y_hx - half_y * ((ez[0] - az) - (ay_z - ay))
@@ -406,9 +619,9 @@
         for c, value in enumerate((ex, ey, ez)):
             spectra_out[c] = spec_from[c] + value * full_c
             spectra_out[6 + c] = spec_from[6 + c] - value * full_s
-        spec_from = spectra_out
-    for c, value in enumerate((ex, ey, ez, hx, hy, hz)):
-        fields_out[c] = value
+        for c, value in enumerate((ex, ey, ez, hx, hy, hz)):
+            fields_out[c] = value
+        return y_hx, y_hz, z_hx, z_hy, x_hy, x_hz
 
     own_walls = walls.at[gz]
     lane_block = iota((8, LANES), 1) // PATCH
@@ -421,24 +634,25 @@
         for c in range(8):
             k = c % 4
             from_c = X_PICKS[k] + (6 if c >= 4 else 0)
-            column = jnp.sum(jnp.where(lane == x_wall, spectra_out[from_c, y], 0.0), axis=1, keepdims=True)
+            column = jnp.where(lane == x_wall, spectra[from_c, y], 0.0) + jnp.where(lane == 8 * (depth + y) + 4, sums[c], 0.0)
+            column = jnp.sum(column, axis=1, keepdims=True)
             spread = jnp.where(lane == c * PATCH + z_row, column * (CURRENT_SIGNS[k] * facing_x), spread)
         record = jnp.sum(spread, axis=0, keepdims=True)
         own_walls[pl.ds(y, 1), :] = record
         for c in range(8):
             k = c % 4
             from_c = Z_PICKS[k] + (6 if c >= 4 else 0)
-            low = spectra_out[from_c, y, pl.ds(ZB, 1), :]
-            high = spectra_out[from_c, y, pl.ds(size_z - 1 - ZB, 1), :]
-            picked = jnp.where(gz == 0, low, high) * (CURRENT_SIGNS[k] * facing_z * end_weight)
+            low = spectra[from_c, y, pl.ds(ZB, 1), :]
+            high = spectra[from_c, y, pl.ds(size_z - 1 - ZB, 1), :]
+            picked = (jnp.where(gz == 0, low, high) + cap_sum[pl.ds(8 * y + c, 1), :]) * (CURRENT_SIGNS[k] * facing_z * end_weight)
             cap_plane[pl.ds(8 * y + c, 1), :] = picked
         wall_hi, wall_lo = split(jnp.where(own_block, record, 0.0) * norm)
         cap_hi, cap_lo = split(cap_plane[pl.ds(8 * y, 8), :] * norm)
-        none = jnp.zeros((8, LANES), BF16)
+        nil = jnp.zeros((8, LANES), BF16)
         for at, (cap_part, wall_part) in enumerate(((cap_hi, wall_hi), (cap_lo, wall_lo))):
             first = at * all_rows + 8 * y
-            lhs[pl.ds(first, 8), :] = jnp.concatenate([cap_part, none], axis=1)
-            lhs[pl.ds(first + half_rows, 8), :] = jnp.concatenate([none, wall_part], axis=1)
+            lhs[pl.ds(first, 8), :] = jnp.concatenate([cap_part, nil], axis=1)
+            lhs[pl.ds(first + half_rows, 8), :] = jnp.concatenate([nil, wall_part], axis=1)
 
     lanes8 = iota((1, LANES), 1)
     owner_row = jnp.zeros((1, LANES), F32)
@@ -560,6 +774,8 @@
             device_id_type=MESH,
         )
 
+    ghosts = advance(0, None)
+
     @pl.when(leads)
     def _():
         everyone = parts_in.at[pl.ds(0, peers - 1)]
@@ -657,9 +873,11 @@
         return total
 
     rounds = owners // together
+    ghosts = advance(1, ghosts)
     choose_owned()
     gradient = lax.fori_loop(0, rounds, adjoint_some, jnp.zeros((all_rows, size_x + 8 * size_z), F32))
     intensity_out[...] = intensity_of(totals[me // ratio])
+    advance(2, ghosts)
     for y in range(size_y):
         wall = gradient[half_rows + 8 * y : half_rows + 8 * y + 8, size_x:]
         adjoint_out[pl.ds(y, 1), 0, :] = jnp.sum(jnp.where(own_block, wall, 0.0), axis=0, keepdims=True) * norm
@@ -670,6 +888,11 @@
         @pl.when(within(move, 1))
         def _():
             halo_copy(0, number, landing, landing).wait_send()
+
+    for number in range(len(regions)):
+        @pl.when(region_when(number, 1))
+        def _():
+            region_copy(number).wait_send()
 
     def parts_sent(ref):
         pltpu.make_async_remote_copy(
@@ -705,7 +928,7 @@
     slabs, devs, xys = (lax.axis_size(a) for a in ("gz", "dev", "xy"))
     peers = slabs * devs * xys
     size_y, size_z, size_x = permittivity.shape
-    assert size_z == PATCH and size_x == LANES and size_y == 4
+    assert size_z == PATCH and size_x == LANES and size_y == 4 and xys == 2
     directions = dir_index.shape[0]
     chunks = directions // LANES
     ratio = peers // chunks
@@ -741,7 +964,16 @@
             *(pltpu.VMEM(shape, F32) for shape in halos),
             pltpu.VMEM((5, size_z, LANES), F32),
             pltpu.VMEM((5, size_y, 1, LANES), F32),
-            pltpu.VMEM((arrival_rows(0, size_y, size_z), 1, LANES), F32),
+            pltpu.VMEM((376, 1, LANES), F32),
+            pltpu.VMEM((2, size_z, LANES), F32),
+            pltpu.VMEM((2, 8, LANES), F32),
+            pltpu.VMEM((3, 2, size_z + 16, LANES), F32),
+            pltpu.VMEM((3, 2, 2, 8, LANES), F32),
+            pltpu.VMEM((2, 3, 3, 8, LANES), F32),
+            pltpu.VMEM((2, 3, 3, 8, LANES), F32),
+            pltpu.VMEM((2, 2, 8, LANES), F32),
+            pltpu.VMEM((3, 3, 8, LANES), F32),
+            pltpu.VMEM((8 * size_y, LANES), F32),
             pltpu.VMEM(fields.shape, F32),
             pltpu.VMEM(spectra.shape, F32),
             pltpu.VMEM(permittivity.shape, F32),
@@ -768,7 +1000,7 @@
             dma, dma((owners // max(1, 4 // per),)),
             dma, dma,
             dma, dma((2,)),
-            dma((9,)), pltpu.SemaphoreType.REGULAR((2,)),
+            dma((9,)), pltpu.SemaphoreType.REGULAR((2,)), dma((19,)), dma((2,)),
         ],
         compiler_params=pltpu.CompilerParams(collective_id=0, has_side_effects=True),
     )(

time: 26.4 us -> 23.1 us (0.88)
  Pallas kernels: 25 us -> 21.7 us
    pallas_call x1, Pallas kernels: 24.1 us -> 20.8 us  [local(): pl.pallas_call(functools.partial(kernel, (slabs, devs, xys)), out_shape=(...]
where the time goes in v4:
time: 23.1 us; the launch traced here: 23 us
  Pallas kernels  21.7 us (94%)
  between operations  1.29 us (6%)
    pallas_call x1, Pallas kernels, local(): pl.pallas_call(functools.partial(kernel, (slabs, devs, xys)), out_shape=(...  20.8 us
    pallas_call x1, Pallas kernels, local(): pl.pallas_call(write_out, out_shape=tuple((jax.ShapeDtypeStruct(shape, F3...  0.86 us

profile of v4, /device:TPU:0, one launch (start us, length us, event | category | flops | bytes accessed | tf_op | source)
XLA Modules:
  0.0 23.0 jit_solution(12191176287776840739)
XLA Ops:
  1.3 20.8 %shard_map.128 = (f32[6,4,16,128]{3,2,1,0:T(8,128)S(1)}, f32[12,4,16,128]{3,2,1,0:T(8,128)S(1)}, f32[20,1,128]{2,1,0:T(1,128)S(1)}, f32[1,128]{1,0:T(1,128)S(1)}, f32[36,1,128]{2,1,0:T(1,128)S(1)}) custom-call(f32[6,4,16,128]{3,2,1,0:T(8,128)} %fields_in.1, f32[12,4,16,128]{3,2,1,0:T(8,128)} %spectra_in.1, f32[4,16,128]{2,1,0:T(8,128)} %permit_in.1, ...), custom_call_target="tpu_custom_call" | custom-call | tf_op jit(solution)/shard_map/pallas_call | solution.py:951
  22.1 0.9 %shard_map.129 = (f32[6,4,16,128]{3,2,1,0:T(8,128)}, f32[12,4,16,128]{3,2,1,0:T(8,128)}, f32[20,1,128]{2,1,0:T(1,128)}, f32[1,128]{1,0:T(1,128)}, f32[36,1,128]{2,1,0:T(1,128)}) custom-call(f32[6,4,16,128]{3,2,1,0:T(8,128)S(1)} %get-tuple-element.15.refs_0_, f32[12,4,16,128]{3,2,1,0:T(8,128)S(1)} %get-tuple-element.16.refs_1_, ...), custom_call_target="tpu_custom_call" | custom-call | tf_op jit(solution)/shard_map/pallas_call | solution.py:1011

commit v5 on v4

--- a/solution.py
+++ b/solution.py
@@ -49,6 +49,13 @@
     return (length + 2) * (size_z + size_y) + 1 + 3 * 8 + 4 * size_z
 
 
+def stagger(tile, by):
+    row = iota(tile.shape, 0)
+    for bit in (1, 2, 4):
+        tile = jnp.where(row // bit % 2 == 1, pltpu.roll(tile, by * bit % LANES, 1), tile)
+    return tile
+
+
 def block_transpose(tile):
     on_diagonal = (iota(tile.shape, 1) // PATCH) == iota(tile.shape, 0)
     total = jnp.where(on_diagonal, tile, 0.0)
@@ -68,7 +75,7 @@
     fields, spectra, permit, phase, wall_owner, cap_owner, dirs, target, aim,
     geo, weights, phases, table_hi, table_lo, cap_plane, lhs,
     parts_out, parts_in, totals, walls, caps,
-    halo_send, halo_got, part_send, part_got, total_send, total_got, wall_send, wall_got, cap_send, cap_got, loads, chain, region_send, region_got,
+    halo_send, halo_got, part_send, part_got, total_send, total_got, wall_send, wall_got, cap_send, cap_got, loads, chain, region_got,
 ):
     slabs, devs, xys = sizes
     peers = slabs * devs * xys
@@ -172,8 +179,8 @@
             z_high, z_low = split(z_part)
             table_hi[j, pl.ds(0, size_x), lanes] = x_high
             table_lo[j, pl.ds(0, size_x), lanes] = x_low
-            table_hi[j, pl.ds(size_x, 8 * size_z), lanes] = jnp.concatenate([z_high] * 8, axis=0)
-            table_lo[j, pl.ds(size_x, 8 * size_z), lanes] = jnp.concatenate([z_low] * 8, axis=0)
+            table_hi[j, pl.ds(size_x, size_z), lanes] = z_high
+            table_lo[j, pl.ds(size_x, size_z), lanes] = z_low
         which = iota((groups, LANES), 0)
         cell_y = (which % size_y).astype(F32) + y_first
         sin_g, cos_g = sincos(cell_y * uy + jnp.where(which < size_y, z_face * uz, x_face * ux))
@@ -345,19 +352,28 @@
         for flip in (0, 1):
             if a or flip:
                 to = {"dev": a, "flip": flip}
-                regions.append((1, to, out_x, land_x.at[1 - a, xy], land_x.at[1 - a, (xy + flip) % 2], empty.at[0, pl.ds(0, 2)]))
+                regions.append((1, to, out_x, land_x.at[1 - a, xy], land_x.at[1 - a, (xy + flip) % 2], empty.at[0, 0]))
     for at, a in enumerate((1, -1)):
         three = pl.ds(size_y - depth, depth) if a > 0 else pl.ds(0, depth)
         two = pl.ds(size_y - 2, 2) if a > 0 else pl.ds(0, 2)
         h_planes = three if a > 0 else two
         h_landing = cap_h.at[at] if a > 0 else cap_h.at[at, :, two]
         tile = pl.ds(zt, 8)
-        for source, landing, nothing in (
-            (fields_in.at[pl.ds(0, 3), three, tile], cap_e.at[at], empty),
-            (fields_in.at[pl.ds(3, 3), h_planes, tile], h_landing, empty if a > 0 else empty.at[:, two]),
-            (permit_in.at[two, tile], cap_r.at[at], empty.at[0, pl.ds(0, 2)]),
+        for kind, source, landing, nothing in (
+            (2, fields_in.at[pl.ds(0, 3), three, tile], cap_e.at[at], empty),
+            (3, fields_in.at[pl.ds(3, 3), h_planes, tile], h_landing, empty if a > 0 else empty.at[:, two]),
+            (3, permit_in.at[two, tile], cap_r.at[at], empty.at[0, pl.ds(0, 2)]),
         ):
-            regions.append((2, {"dev": a}, source, landing, landing, nothing))
+            regions.append((kind, {"dev": a}, source, landing, landing, nothing))
+
+    def group_of(number):
+        kind, move = regions[number][:2]
+        if kind:
+            return len(messages) + 2 + (0 if not move["dev"] else 1 if move["dev"] > 0 else 2)
+        for at, (_, other) in enumerate(messages):
+            if {axis: step for axis, step in move.items() if step} == other:
+                return at
+        return len(messages) + (0 if move["dev"] > 0 else 1)
 
     def region_inside(move, sign):
         return within({axis: step for axis, step in move.items() if axis != "flip" and step}, sign)
@@ -370,8 +386,8 @@
         return pltpu.make_async_remote_copy(
             src_ref=source,
             dst_ref=landing,
-            send_sem=region_send.at[number],
-            recv_sem=region_got.at[min(kind, 1)],
+            send_sem=halo_send.at[group_of(number)],
+            recv_sem=region_got.at[min(kind, 2)],
             device_id=to,
             device_id_type=MESH,
         )
@@ -393,10 +409,10 @@
 
             @pl.when(jnp.logical_and(missing, is_end) if kind else missing)
             def _():
-                pltpu.make_async_copy(nothing, landing, region_got.at[min(kind, 1)]).start()
+                pltpu.make_async_copy(nothing, landing, region_got.at[min(kind, 2)]).start()
 
     def wait_region(which):
-        length = (10 * size_z) if which == 0 else 80 + 296
+        length = (10 * size_z, 5 * 8, 2 * 9 * 8 + (9 + 6) * 8 + 2 * 2 * 8)[which]
         everything = arrivals.at[pl.ds(0, length)]
         pltpu.make_async_copy(everything, everything, region_got.at[which]).wait()
 
@@ -415,6 +431,7 @@
         return packs
 
     empty[...] = jnp.zeros(empty.shape, F32)
+    lhs[...] = jnp.zeros(lhs.shape, BF16)
     pl.semaphore_wait(barrier, beside)
     start_regions((2,))
     pass_on()
@@ -425,23 +442,28 @@
     for part in range(2):
         out_w[part] = own[part]
         land_w[1, part, pl.ds(8, size_z), :] = own[part]
+    start_regions((0,))
 
     @pl.when(is_end)
     def _():
         tile = pl.ds(zt, 8)
-        packs = window([fields[c, :, tile, :] for c in range(6)] + [permit[:, tile, :]], lambda base: (base + 4) % LANES)
-        left = iota((8, LANES), 1) % 8 < 4
-        mine_half = jnp.where(xy == 0, 1.0, 0.0)
-        for part in range(2):
-            kept = packs[part] * jnp.where(left, mine_half, 1.0 - mine_half)
-            out_x[part] = kept
-            land_x[1, xy, part] = kept
+        eight = iota((8, LANES), 1)
+        packed = jnp.full((8, LANES), COURANT, F32)
+        for c in range(7):
+            values = permit[:, tile, :] if c == 6 else fields[c, :, tile, :]
+            for y in range(size_y):
+                base = quarter * (c % 4) + 8 * y + 4 * (c // 4)
+                turned = pltpu.roll(values[y], (base + 4 * (1 - xy)) % LANES, 1)
+                packed = jnp.where(jnp.logical_and(eight >= base, eight < base + 4), turned, packed)
+        out_x[...] = packed
+        land_x[1, xy] = packed
 
     @pl.when(jnp.logical_not(is_end))
     def _():
         land_x[...] = jnp.zeros(land_x.shape, F32)
 
-    start_regions((1, 0))
+    start_regions((1,))
+    start_regions((3,))
     for _ in stage(0, *(fields[c] for c in range(3)), (fields[3], fields[5]), (fields[3], fields[4]), (fields[4], fields[5])):
         pass
     start_halo(0, (4, 5, 8, 11, 9, 10, 0, 1, 2, 3, 6, 7))
@@ -477,21 +499,23 @@
         wait_region(1)
 
     tall = size_z + 16
-    spot = iota((tall + 8, LANES), 1)
-    joined = [
-        [jnp.concatenate([land_w[dy, part], land_x[dy, 0, part] + land_x[dy, 1, part]], axis=0) for part in range(2)]
-        for dy in range(3)
-    ]
+    low_spot = iota((tall, LANES), 1)
+    high_spot = iota((8, LANES), 1)
     held = []
     for c in range(8):
-        value = jnp.zeros((tall + 8, LANES), F32)
+        value = jnp.zeros((tall, LANES), F32)
+        border = jnp.zeros((8, LANES), F32)
         first = 0
         for dy, planes in enumerate((depth, size_y, depth)):
             start = quarter * (c % 4) + (8 * (size_y - depth) if dy == 0 else 0)
-            chosen = jnp.logical_and(spot >= first, spot < first + 8 * planes)
-            value = jnp.where(chosen, turn(joined[dy][c // 4], first - start, 1), value)
-            first += 8 * planes
-        held.append(value)
+            last = first + 8 * planes
+            chosen = jnp.logical_and(low_spot >= first, low_spot < last)
+            value = jnp.where(chosen, turn(land_w[dy, c // 4], first - start, 1), value)
+            for side in range(2):
+                chosen = jnp.logical_and(jnp.logical_and(high_spot >= first, high_spot < last), high_spot % 8 // 4 == side)
+                border = jnp.where(chosen, turn(land_x[dy, side], first - start - 4 * (c // 4) + 4 * side, 1), border)
+            first = last
+        held.append(jnp.concatenate([value, border], axis=0))
     ex, ey, ez, hx, hy, hz, r, k = held
     border_e, border_h = [], []
     sums = [jnp.zeros((size_z, LANES), F32) for _ in range(8)]
@@ -513,6 +537,7 @@
 
     @pl.when(is_end)
     def _():
+        wait_region(2)
         tile = pl.ds(zt, 8)
         eight = iota((8, LANES), 1)
         left, right = jnp.where(xy == 0, 1.0, 0.0), jnp.where(xy == 0, 0.0, 1.0)
@@ -624,9 +649,7 @@
         return y_hx, y_hz, z_hx, z_hy, x_hy, x_hz
 
     own_walls = walls.at[gz]
-    lane_block = iota((8, LANES), 1) // PATCH
     sub = iota((8, LANES), 0)
-    own_block = lane_block == sub
     z_row = iota((size_z, LANES), 0)
     own_walls[...] = jnp.zeros((8, LANES), F32)
     for y in range(size_y):
@@ -646,13 +669,13 @@
             high = spectra[from_c, y, pl.ds(size_z - 1 - ZB, 1), :]
             picked = (jnp.where(gz == 0, low, high) + cap_sum[pl.ds(8 * y + c, 1), :]) * (CURRENT_SIGNS[k] * facing_z * end_weight)
             cap_plane[pl.ds(8 * y + c, 1), :] = picked
-        wall_hi, wall_lo = split(jnp.where(own_block, record, 0.0) * norm)
+        fanned = stagger(jnp.broadcast_to(record, (8, LANES)), -PATCH)
+        wall_hi, wall_lo = split(fanned[:, :size_z] * norm)
         cap_hi, cap_lo = split(cap_plane[pl.ds(8 * y, 8), :] * norm)
-        nil = jnp.zeros((8, LANES), BF16)
         for at, (cap_part, wall_part) in enumerate(((cap_hi, wall_hi), (cap_lo, wall_lo))):
             first = at * all_rows + 8 * y
-            lhs[pl.ds(first, 8), :] = jnp.concatenate([cap_part, nil], axis=1)
-            lhs[pl.ds(first + half_rows, 8), :] = jnp.concatenate([nil, wall_part], axis=1)
+            lhs[pl.ds(first, 8), pl.ds(0, size_x)] = cap_part
+            lhs[pl.ds(first + half_rows, 8), pl.ds(size_x, size_z)] = wall_part
 
     lanes8 = iota((1, LANES), 1)
     owner_row = jnp.zeros((1, LANES), F32)
@@ -853,7 +876,7 @@
         by_low = lax.dot_general(high, table_lo[j], across, preferred_element_type=F32)
         return by_high[:all_rows] + by_high[all_rows:] + by_low
 
-    def adjoint_some(number, total):
+    def adjoint_wait(number):
         several = [partner(together * number + m) for m in range(together)]
         batch = several[0] // together
         ours = jnp.logical_and(leads, mine // together == batch)
@@ -867,6 +890,10 @@
             def _():
                 total_copy(1, several[0], totals.at[pl.ds(batch * bunch, bunch - per)]).wait_recv()
 
+        return several
+
+    def adjoint_some(numbers, total):
+        several = [owner for number in numbers for owner in adjoint_wait(number)]
         for owner in several:
             for m in range(per):
                 total = total + adjoint_of(owner * per + m)
@@ -875,24 +902,29 @@
     rounds = owners // together
     ghosts = advance(1, ghosts)
     choose_owned()
-    gradient = lax.fori_loop(0, rounds, adjoint_some, jnp.zeros((all_rows, size_x + 8 * size_z), F32))
+    gradient = adjoint_some((0,), jnp.zeros((all_rows, size_x + size_z), F32))
+    gradient = adjoint_some(range(1, rounds), gradient)
     intensity_out[...] = intensity_of(totals[me // ratio])
     advance(2, ghosts)
     for y in range(size_y):
         wall = gradient[half_rows + 8 * y : half_rows + 8 * y + 8, size_x:]
-        adjoint_out[pl.ds(y, 1), 0, :] = jnp.sum(jnp.where(own_block, wall, 0.0), axis=0, keepdims=True) * norm
+        wall = jnp.concatenate([wall, jnp.zeros((8, LANES - size_z), F32)], axis=1)
+        wall = stagger(wall, PATCH)
+        adjoint_out[pl.ds(y, 1), 0, :] = jnp.sum(wall, axis=0, keepdims=True) * norm
         cap = block_transpose(gradient[8 * y : 8 * y + 8, :size_x] * (norm * end_weight))
         adjoint_out[pl.ds(size_y + 8 * y, 8), 0, :] = cap
 
+    groups_sent = {}
     for number, (landing, move) in enumerate(messages):
-        @pl.when(within(move, 1))
+        groups_sent[number] = [within(move, 1), math.prod(landing.shape) // LANES]
+    for number, (_, _, source, _, _, _) in enumerate(regions):
+        entry = groups_sent.setdefault(group_of(number), [region_when(number, 1), 0])
+        entry[1] += math.prod(source.shape) // LANES
+    for group, (sent, rows_sent) in groups_sent.items():
+        @pl.when(sent)
         def _():
-            halo_copy(0, number, landing, landing).wait_send()
-
-    for number in range(len(regions)):
-        @pl.when(region_when(number, 1))
-        def _():
-            region_copy(number).wait_send()
+            everything = arrivals.at[pl.ds(0, rows_sent)]
+            pltpu.make_async_copy(everything, everything, halo_send.at[group]).wait()
 
     def parts_sent(ref):
         pltpu.make_async_remote_copy(
@@ -938,7 +970,7 @@
     cap_count = size_y * size_x // PATCH
     owned = size_y + 2 * (cap_count // slabs)
     rows = 16 * size_y
-    depth = size_x + 8 * size_z
+    depth = size_x + size_z
     planes, pairs = 5 + 3 * (STEPS - 1), 2 * STEPS
     halos = (
         (planes, size_z, LANES), (pairs, size_z, LANES), (planes, size_y, 1, LANES), (pairs, size_y, 1, LANES),
@@ -966,9 +998,9 @@
             pltpu.VMEM((5, size_y, 1, LANES), F32),
             pltpu.VMEM((376, 1, LANES), F32),
             pltpu.VMEM((2, size_z, LANES), F32),
-            pltpu.VMEM((2, 8, LANES), F32),
+            pltpu.VMEM((8, LANES), F32),
             pltpu.VMEM((3, 2, size_z + 16, LANES), F32),
-            pltpu.VMEM((3, 2, 2, 8, LANES), F32),
+            pltpu.VMEM((3, 2, 8, LANES), F32),
             pltpu.VMEM((2, 3, 3, 8, LANES), F32),
             pltpu.VMEM((2, 3, 3, 8, LANES), F32),
             pltpu.VMEM((2, 2, 8, LANES), F32),
@@ -995,12 +1027,12 @@
             pltpu.VMEM((chunks, 4, LANES), F32),
             pltpu.VMEM((slabs, 8, LANES), F32),
             pltpu.VMEM((2, cap_count, LANES), F32),
-            dma((len(halos),)), dma((STEPS,)),
+            dma((len(halos) + 5,)), dma((STEPS,)),
             dma, dma,
             dma, dma((owners // max(1, 4 // per),)),
             dma, dma,
             dma, dma((2,)),
-            dma((9,)), pltpu.SemaphoreType.REGULAR((2,)), dma((19,)), dma((2,)),
+            dma((9,)), pltpu.SemaphoreType.REGULAR((2,)), dma((3,)),
         ],
         compiler_params=pltpu.CompilerParams(collective_id=0, has_side_effects=True),
     )(

time: 23.1 us -> 22.2 us (0.961)
  Pallas kernels: 21.7 us -> 20.7 us
    pallas_call x1, Pallas kernels: 20.8 us -> 19.9 us  [local(): pl.pallas_call(functools.partial(kernel, (slabs, devs, xys)), out_shape=(...]
where the time goes in v5:
time: 22.2 us; the launch traced here: 22 us
  Pallas kernels  20.7 us (93%)
  between operations  1.29 us (6%)
    pallas_call x1, Pallas kernels, local(): pl.pallas_call(functools.partial(kernel, (slabs, devs, xys)), out_shape=(...  19.9 us
    pallas_call x1, Pallas kernels, local(): pl.pallas_call(write_out, out_shape=tuple((jax.ShapeDtypeStruct(shape, F3...  0.86 us

profile of v5, /device:TPU:0, one launch (start us, length us, event | category | flops | bytes accessed | tf_op | source)
XLA Modules:
  0.0 22.0 jit_solution(17345756450181152413)
XLA Ops:
  1.3 19.9 %shard_map.128 = (f32[6,4,16,128]{3,2,1,0:T(8,128)S(1)}, f32[12,4,16,128]{3,2,1,0:T(8,128)S(1)}, f32[20,1,128]{2,1,0:T(1,128)S(1)}, f32[1,128]{1,0:T(1,128)S(1)}, f32[36,1,128]{2,1,0:T(1,128)S(1)}) custom-call(f32[6,4,16,128]{3,2,1,0:T(8,128)} %fields_in.1, f32[12,4,16,128]{3,2,1,0:T(8,128)} %spectra_in.1, f32[4,16,128]{2,1,0:T(8,128)} %permit_in.1, ...), custom_call_target="tpu_custom_call" | custom-call | tf_op jit(solution)/shard_map/pallas_call | solution.py:983
  21.1 0.9 %shard_map.129 = (f32[6,4,16,128]{3,2,1,0:T(8,128)}, f32[12,4,16,128]{3,2,1,0:T(8,128)}, f32[20,1,128]{2,1,0:T(1,128)}, f32[1,128]{1,0:T(1,128)}, f32[36,1,128]{2,1,0:T(1,128)}) custom-call(f32[6,4,16,128]{3,2,1,0:T(8,128)S(1)} %get-tuple-element.15.refs_0_, f32[12,4,16,128]{3,2,1,0:T(8,128)S(1)} %get-tuple-element.16.refs_1_, ...), custom_call_target="tpu_custom_call" | custom-call | tf_op jit(solution)/shard_map/pallas_call | solution.py:1043

commit v6 on v5

--- a/solution.py
+++ b/solution.py
@@ -360,8 +360,8 @@
         h_landing = cap_h.at[at] if a > 0 else cap_h.at[at, :, two]
         tile = pl.ds(zt, 8)
         for kind, source, landing, nothing in (
-            (2, fields_in.at[pl.ds(0, 3), three, tile], cap_e.at[at], empty),
-            (3, fields_in.at[pl.ds(3, 3), h_planes, tile], h_landing, empty if a > 0 else empty.at[:, two]),
+            (2, fields.at[pl.ds(0, 3), three, tile], cap_e.at[at], empty),
+            (3, fields.at[pl.ds(3, 3), h_planes, tile], h_landing, empty if a > 0 else empty.at[:, two]),
             (3, permit_in.at[two, tile], cap_r.at[at], empty.at[0, pl.ds(0, 2)]),
         ):
             regions.append((kind, {"dev": a}, source, landing, landing, nothing))
@@ -433,9 +433,9 @@
     empty[...] = jnp.zeros(empty.shape, F32)
     lhs[...] = jnp.zeros(lhs.shape, BF16)
     pl.semaphore_wait(barrier, beside)
-    start_regions((2,))
     pass_on()
     loading[0].wait()
+    start_regions((2,))
     loading[3].wait()
     permit[...] = COURANT / permit[...]
     own = window([fields[c] for c in range(6)] + [permit[...]], lambda base: (base - (x_wall - 4) + 2 * LANES) % LANES)
@@ -492,48 +492,95 @@
     def full_of(n):
         return run_c[2 * n + 1 : 2 * n + 2, :], run_s[2 * n + 1 : 2 * n + 2, :]
 
+    cap_sum[...] = jnp.zeros(cap_sum.shape, F32)
+    own_walls = walls.at[gz]
+    own_walls[...] = jnp.zeros((8, LANES), F32)
+    lanes8 = iota((1, LANES), 1)
+    owner_row = jnp.zeros((1, LANES), F32)
+    for p in range(size_y):
+        owner_row = jnp.where(lanes8 == 8 * gz + p, (wall_owner[0, p] + 1).astype(F32), owner_row)
+    own_walls[pl.ds(size_y, 1), :] = owner_row
+    gathered = jnp.zeros((size_z, LANES), F32)
+    for y in range(size_y):
+        for c in range(8):
+            k = c % 4
+            from_c = X_PICKS[k] + (6 if c >= 4 else 0)
+            turned = pltpu.roll(spectra[from_c, y], (8 * y + c - x_wall + 2 * LANES) % LANES, 1)
+            gathered = jnp.where(lane == 8 * y + c, turned, gathered)
+            from_c = Z_PICKS[k] + (6 if c >= 4 else 0)
+            low = spectra[from_c, y, pl.ds(ZB, 1), :]
+            high = spectra[from_c, y, pl.ds(size_z - 1 - ZB, 1), :]
+            cap_plane[pl.ds(8 * y + c, 1), :] = jnp.where(gz == 0, low, high)
+
+    def spread_out(source_of, rows, shift_of, masks):
+        spot = iota((rows, LANES), 1)
+        values = []
+        for c in range(8):
+            value = jnp.zeros((rows, LANES), F32)
+            first = 0
+            for dy, planes in enumerate((depth, size_y, depth)):
+                start = quarter * (c % 4) + (8 * (size_y - depth) if dy == 0 else 0)
+                last = first + 8 * planes
+                inside = jnp.logical_and(spot >= first, spot < last)
+                for side in range(masks):
+                    chosen = inside if masks == 1 else jnp.logical_and(inside, spot % 8 // 4 == side)
+                    value = jnp.where(chosen, turn(source_of(dy, c, side), first - start + shift_of(c, side), 1), value)
+                first = last
+            values.append(value)
+        return values
+
+    def steps_of(values, visit):
+        ex, ey, ez, hx, hy, hz, r, k = values
+        for n in range(STEPS):
+            before = (ez, ey)
+            hx = hx - k * ((turn(ez, -8, 1) - ez) - (turn(ey, -1, 0) - ey))
+            hy = hy - k * ((turn(ex, -1, 0) - ex) - (turn(ez, -1, 1) - ez))
+            hz = hz - k * ((turn(ey, -1, 1) - ey) - (turn(ex, -8, 1) - ex))
+            ex = ex + r * ((hz - turn(hz, 8, 1)) - (hy - turn(hy, 1, 0)))
+            ey = ey + r * ((hx - turn(hx, 1, 0)) - (hz - turn(hz, 1, 1)))
+            ez = ez + r * ((hy - turn(hy, 1, 1)) - (hx - turn(hx, 8, 1)))
+            visit(n, before, ey, ez, hy, hz)
+
     wait_region(0)
 
     @pl.when(is_end)
     def _():
         wait_region(1)
 
-    tall = size_z + 16
-    low_spot = iota((tall, LANES), 1)
-    high_spot = iota((8, LANES), 1)
-    held = []
-    for c in range(8):
-        value = jnp.zeros((tall, LANES), F32)
-        border = jnp.zeros((8, LANES), F32)
-        first = 0
-        for dy, planes in enumerate((depth, size_y, depth)):
-            start = quarter * (c % 4) + (8 * (size_y - depth) if dy == 0 else 0)
-            last = first + 8 * planes
-            chosen = jnp.logical_and(low_spot >= first, low_spot < last)
-            value = jnp.where(chosen, turn(land_w[dy, c // 4], first - start, 1), value)
-            for side in range(2):
-                chosen = jnp.logical_and(jnp.logical_and(high_spot >= first, high_spot < last), high_spot % 8 // 4 == side)
-                border = jnp.where(chosen, turn(land_x[dy, side], first - start - 4 * (c // 4) + 4 * side, 1), border)
-            first = last
-        held.append(jnp.concatenate([value, border], axis=0))
-    ex, ey, ez, hx, hy, hz, r, k = held
-    border_e, border_h = [], []
     sums = [jnp.zeros((size_z, LANES), F32) for _ in range(8)]
-    for n in range(STEPS):
-        border_e.append((ez[tall:], ey[tall:]))
-        hx = hx - k * ((turn(ez, -8, 1) - ez) - (turn(ey, -1, 0) - ey))
-        hy = hy - k * ((turn(ex, -1, 0) - ex) - (turn(ez, -1, 1) - ez))
-        hz = hz - k * ((turn(ey, -1, 1) - ey) - (turn(ex, -8, 1) - ex))
-        border_h.append((hz[tall:], hy[tall:]))
-        ex = ex + r * ((hz - turn(hz, 8, 1)) - (hy - turn(hy, 1, 0)))
-        ey = ey + r * ((hx - turn(hx, 1, 0)) - (hz - turn(hz, 1, 1)))
-        ez = ez + r * ((hy - turn(hy, 1, 1)) - (hx - turn(hx, 8, 1)))
+
+    def add_up(n, before, ey, ez, hy, hz):
         for at, (value, (co, si)) in enumerate(((hz, half_of(n)), (hy, half_of(n)), (ez, full_of(n)), (ey, full_of(n)))):
-            value = value[8 : 8 + size_z]
+            value = value[:size_z]
             sums[at] = sums[at] + value * co
             sums[4 + at] = sums[4 + at] - value * si
 
-    cap_sum[...] = jnp.zeros(cap_sum.shape, F32)
+    folded = [
+        [
+            jnp.concatenate([
+                land_w[dy, part, pl.ds(8, size_z), :],
+                jnp.where(iota((8, LANES), 0) < 4, land_w[dy, part, pl.ds(size_z + 8, 8), :], land_w[dy, part, pl.ds(0, 8), :]),
+            ], axis=0)
+            for part in range(2)
+        ]
+        for dy in range(3)
+    ]
+    border_e, border_h = [], []
+
+    def keep(n, before, ey, ez, hy, hz):
+        border_e.append(before)
+        border_h.append((hz, hy))
+
+    steps_of(spread_out(lambda dy, c, side: folded[dy][c // 4], size_z + 8, lambda c, side: 0, 1), add_up)
+    steps_of(spread_out(lambda dy, c, side: land_x[dy, side], 8, lambda c, side: 4 * side - 4 * (c // 4), 2), keep)
+    for c in range(8):
+        chosen = jnp.logical_and(lane % 8 == c, lane < 8 * size_y)
+        gathered = gathered + jnp.where(chosen, turn(sums[c], c - 8 * depth - 4, 1), 0.0)
+    row_sign = jnp.where(jnp.logical_and(iota((half_rows, LANES), 0) % 4 > 0, iota((half_rows, LANES), 0) % 4 < 3), 1.0, -1.0)
+    wall_cells = jnp.transpose(gathered)[:half_rows] * (row_sign[:, :size_z] * facing_x)
+    for at, part in enumerate(split(wall_cells * norm)):
+        lhs[pl.ds(at * all_rows + half_rows, half_rows), pl.ds(size_x, size_z)] = part
+
 
     @pl.when(is_end)
     def _():
@@ -648,40 +695,11 @@
             fields_out[c] = value
         return y_hx, y_hz, z_hx, z_hy, x_hy, x_hz
 
-    own_walls = walls.at[gz]
     sub = iota((8, LANES), 0)
-    z_row = iota((size_z, LANES), 0)
-    own_walls[...] = jnp.zeros((8, LANES), F32)
-    for y in range(size_y):
-        spread = jnp.zeros((size_z, LANES), F32)
-        for c in range(8):
-            k = c % 4
-            from_c = X_PICKS[k] + (6 if c >= 4 else 0)
-            column = jnp.where(lane == x_wall, spectra[from_c, y], 0.0) + jnp.where(lane == 8 * (depth + y) + 4, sums[c], 0.0)
-            column = jnp.sum(column, axis=1, keepdims=True)
-            spread = jnp.where(lane == c * PATCH + z_row, column * (CURRENT_SIGNS[k] * facing_x), spread)
-        record = jnp.sum(spread, axis=0, keepdims=True)
-        own_walls[pl.ds(y, 1), :] = record
-        for c in range(8):
-            k = c % 4
-            from_c = Z_PICKS[k] + (6 if c >= 4 else 0)
-            low = spectra[from_c, y, pl.ds(ZB, 1), :]
-            high = spectra[from_c, y, pl.ds(size_z - 1 - ZB, 1), :]
-            picked = (jnp.where(gz == 0, low, high) + cap_sum[pl.ds(8 * y + c, 1), :]) * (CURRENT_SIGNS[k] * facing_z * end_weight)
-            cap_plane[pl.ds(8 * y + c, 1), :] = picked
-        fanned = stagger(jnp.broadcast_to(record, (8, LANES)), -PATCH)
-        wall_hi, wall_lo = split(fanned[:, :size_z] * norm)
-        cap_hi, cap_lo = split(cap_plane[pl.ds(8 * y, 8), :] * norm)
-        for at, (cap_part, wall_part) in enumerate(((cap_hi, wall_hi), (cap_lo, wall_lo))):
-            first = at * all_rows + 8 * y
-            lhs[pl.ds(first, 8), pl.ds(0, size_x)] = cap_part
-            lhs[pl.ds(first + half_rows, 8), pl.ds(size_x, size_z)] = wall_part
-
-    lanes8 = iota((1, LANES), 1)
-    owner_row = jnp.zeros((1, LANES), F32)
-    for p in range(size_y):
-        owner_row = jnp.where(lanes8 == 8 * gz + p, (wall_owner[0, p] + 1).astype(F32), owner_row)
-    own_walls[pl.ds(size_y, 1), :] = owner_row
+    caps_now = (cap_plane[...] + cap_sum[...]) * (row_sign * (facing_z * end_weight))
+    cap_plane[...] = caps_now
+    for at, part in enumerate(split(caps_now * norm)):
+        lhs[pl.ds(at * all_rows, half_rows), pl.ds(0, size_x)] = part
 
     def wall_copy(k, ref=None):
         held = walls.at[gz] if ref is None else ref
@@ -776,6 +794,10 @@
     hear()
     lax.fori_loop(0, owners // together, far_and_send, 0)
 
+    ghosts = advance(0, None)
+    for y in range(size_y):
+        cells = jnp.concatenate([wall_cells[8 * y : 8 * y + 8], jnp.zeros((8, LANES - size_z), F32)], axis=1)
+        own_walls[pl.ds(y, 1), :] = jnp.sum(stagger(cells, PATCH), axis=0, keepdims=True)
     for k in range(1, slabs):
         wall_copy(k).start()
     for at, holder in enumerate((0, slabs - 1)):
@@ -796,8 +818,6 @@
             device_id=ident((me + k) % peers),
             device_id_type=MESH,
         )
-
-    ghosts = advance(0, None)
 
     @pl.when(leads)
     def _():

time: 22.2 us -> 21.6 us (0.973)
  Pallas kernels: 20.7 us -> 20.2 us
    pallas_call x1, Pallas kernels: 19.9 us -> 19.3 us  [local(): pl.pallas_call(functools.partial(kernel, (slabs, devs, xys)), out_shape=(...]
where the time goes in v6:
time: 21.6 us; the launch traced here: 21.5 us
  Pallas kernels  20.2 us (94%)
  between operations  1.29 us (6%)
    pallas_call x1, Pallas kernels, local(): pl.pallas_call(functools.partial(kernel, (slabs, devs, xys)), out_shape=(...  19.3 us
    pallas_call x1, Pallas kernels, local(): pl.pallas_call(write_out, out_shape=tuple((jax.ShapeDtypeStruct(shape, F3...  0.86 us

profile of v6, /device:TPU:0, one launch (start us, length us, event | category | flops | bytes accessed | tf_op | source)
XLA Modules:
  0.0 21.5 jit_solution(16468929668503717483)
XLA Ops:
  1.3 19.3 %shard_map.128 = (f32[6,4,16,128]{3,2,1,0:T(8,128)S(1)}, f32[12,4,16,128]{3,2,1,0:T(8,128)S(1)}, f32[20,1,128]{2,1,0:T(1,128)S(1)}, f32[1,128]{1,0:T(1,128)S(1)}, f32[36,1,128]{2,1,0:T(1,128)S(1)}) custom-call(f32[6,4,16,128]{3,2,1,0:T(8,128)} %fields_in.1, f32[12,4,16,128]{3,2,1,0:T(8,128)} %spectra_in.1, f32[4,16,128]{2,1,0:T(8,128)} %permit_in.1, ...), custom_call_target="tpu_custom_call" | custom-call | tf_op jit(solution)/shard_map/pallas_call | solution.py:1003
  20.6 0.9 %shard_map.129 = (f32[6,4,16,128]{3,2,1,0:T(8,128)}, f32[12,4,16,128]{3,2,1,0:T(8,128)}, f32[20,1,128]{2,1,0:T(1,128)}, f32[1,128]{1,0:T(1,128)}, f32[36,1,128]{2,1,0:T(1,128)}) custom-call(f32[6,4,16,128]{3,2,1,0:T(8,128)S(1)} %get-tuple-element.15.refs_0_, f32[12,4,16,128]{3,2,1,0:T(8,128)S(1)} %get-tuple-element.16.refs_1_, ...), custom_call_target="tpu_custom_call" | custom-call | tf_op jit(solution)/shard_map/pallas_call | solution.py:1063

commit v7 on v6

--- a/solution.py
+++ b/solution.py
@@ -71,11 +71,11 @@
     fields_out, spectra_out, owned_out, intensity_out, adjoint_out,
     out_yu, out_yd, out_zu, out_zd, out_xu, out_xd,
     in_yu, in_yd, in_zu, in_zd, in_xu, in_xd, in_zy, in_yz, in_yx, in_zx, in_xz, in_xy, blank, blank_rows, arrivals,
-    out_w, out_x, land_w, land_x, cap_e, cap_h, cap_r, empty, cap_sum,
+    out_w, out_z, out_x, land_w, land_z, land_x, tile_e, tile_h, tile_f, cap_e, cap_h, cap_f, empty, empty_half, cap_sum,
     fields, spectra, permit, phase, wall_owner, cap_owner, dirs, target, aim,
     geo, weights, phases, table_hi, table_lo, cap_plane, lhs,
     parts_out, parts_in, totals, walls, caps,
-    halo_send, halo_got, part_send, part_got, total_send, total_got, wall_send, wall_got, cap_send, cap_got, loads, chain, region_got,
+    halo_send, halo_got, part_got, total_got, wall_got, cap_send, cap_got, loads, chain, region_got,
 ):
     slabs, devs, xys = sizes
     peers = slabs * devs * xys
@@ -237,12 +237,17 @@
             (out_xu.at[n, low], in_xz.at[n]), (out_xu.at[n], in_xy.at[n]),
         )
 
+    def sent_by(group):
+        if 6 <= group < 12:
+            return loads.at[(1, 2, 4, 5, 6, 7)[group - 6]]
+        return halo_send.at[group if group < 6 else group - 6]
+
     def halo_copy(n, number, source, landing):
         to = {axis: (place[axis] + step + count[axis]) % count[axis] for axis, step in messages[number][1].items()}
         return pltpu.make_async_remote_copy(
             src_ref=source,
             dst_ref=landing,
-            send_sem=halo_send.at[number],
+            send_sem=sent_by(number),
             recv_sem=halo_got.at[n],
             device_id=to,
             device_id_type=MESH,
@@ -337,32 +342,26 @@
     depth = STEPS
     extent = size_y + 2 * depth
     quarter = 8 * size_y
-    low_tile, high_tile = pl.ds(0, 8), pl.ds(size_z - 8, 8)
 
     regions = []
     for a in (1, -1, 0):
         for b in (1, -1, 0):
             if a or b:
-                source = out_w if b == 0 else out_w.at[:, high_tile if b > 0 else low_tile]
-                rows = pl.ds(8, size_z) if b == 0 else pl.ds(0 if b > 0 else size_z + 8, 8)
-                landing = land_w.at[1 - a, :, rows]
-                nothing = blank.at[pl.ds(0, 2)] if b == 0 else empty.at[0, pl.ds(0, 2)]
+                source = out_w if b == 0 else out_z.at[1 if b > 0 else 0]
+                landing = land_w.at[1 - a] if b == 0 else land_z.at[1 - a, 1 if b > 0 else 0]
+                nothing = blank.at[pl.ds(0, 2)] if b == 0 else empty_half.at[pl.ds(0, 2)]
                 regions.append((0, {"dev": a, "gz": b}, source, landing, landing, nothing))
     for a in (1, -1, 0):
         for flip in (0, 1):
             if a or flip:
                 to = {"dev": a, "flip": flip}
-                regions.append((1, to, out_x, land_x.at[1 - a, xy], land_x.at[1 - a, (xy + flip) % 2], empty.at[0, 0]))
+                regions.append((1, to, out_x, land_x.at[1 - a, xy], land_x.at[1 - a, (xy + flip) % 2], empty.at[0]))
     for at, a in enumerate((1, -1)):
-        three = pl.ds(size_y - depth, depth) if a > 0 else pl.ds(0, depth)
-        two = pl.ds(size_y - 2, 2) if a > 0 else pl.ds(0, 2)
-        h_planes = three if a > 0 else two
-        h_landing = cap_h.at[at] if a > 0 else cap_h.at[at, :, two]
-        tile = pl.ds(zt, 8)
+        far_count = 6 if a > 0 else 3
         for kind, source, landing, nothing in (
-            (2, fields.at[pl.ds(0, 3), three, tile], cap_e.at[at], empty),
-            (3, fields.at[pl.ds(3, 3), h_planes, tile], h_landing, empty if a > 0 else empty.at[:, two]),
-            (3, permit_in.at[two, tile], cap_r.at[at], empty.at[0, pl.ds(0, 2)]),
+            (2, tile_e.at[at], cap_e.at[at], empty.at[pl.ds(0, 6)]),
+            (3, tile_h.at[at], cap_h.at[at], empty),
+            (3, tile_f.at[at, pl.ds(0, far_count)], cap_f.at[at, pl.ds(0, far_count)], empty_half.at[pl.ds(0, far_count)]),
         ):
             regions.append((kind, {"dev": a}, source, landing, landing, nothing))
 
@@ -386,7 +385,7 @@
         return pltpu.make_async_remote_copy(
             src_ref=source,
             dst_ref=landing,
-            send_sem=halo_send.at[group_of(number)],
+            send_sem=sent_by(group_of(number)),
             recv_sem=region_got.at[min(kind, 2)],
             device_id=to,
             device_id_type=MESH,
@@ -412,7 +411,7 @@
                 pltpu.make_async_copy(nothing, landing, region_got.at[min(kind, 2)]).start()
 
     def wait_region(which):
-        length = (10 * size_z, 5 * 8, 2 * 9 * 8 + (9 + 6) * 8 + 2 * 2 * 8)[which]
+        length = (4 * size_z + 6 * 8, 5 * 8, 2 * (6 + 8) * 8 + (6 + 3) * 4)[which]
         everything = arrivals.at[pl.ds(0, length)]
         pltpu.make_async_copy(everything, everything, region_got.at[which]).wait()
 
@@ -431,22 +430,46 @@
         return packs
 
     empty[...] = jnp.zeros(empty.shape, F32)
+    empty_half[...] = jnp.zeros(empty_half.shape, F32)
     lhs[...] = jnp.zeros(lhs.shape, BF16)
     pl.semaphore_wait(barrier, beside)
     pass_on()
     loading[0].wait()
+
+    @pl.when(is_end)
+    def _():
+        tile = pl.ds(zt, 8)
+        for c in range(3):
+            for i in range(2):
+                tile_e[0, 2 * c + i] = fields[c, size_y - 2 + i, tile, :]
+                tile_e[1, 2 * c + i] = fields[c, i, tile, :]
+
     start_regions((2,))
     loading[3].wait()
     permit[...] = COURANT / permit[...]
     own = window([fields[c] for c in range(6)] + [permit[...]], lambda base: (base - (x_wall - 4) + 2 * LANES) % LANES)
     for part in range(2):
         out_w[part] = own[part]
-        land_w[1, part, pl.ds(8, size_z), :] = own[part]
+        land_w[1, part] = own[part]
+        out_z[0, part] = own[part][:4]
+        out_z[1, part] = own[part][size_z - 4 :]
     start_regions((0,))
 
     @pl.when(is_end)
     def _():
         tile = pl.ds(zt, 8)
+        for i in range(2):
+            for c in range(3):
+                tile_h[0, 2 * c + i] = fields[3 + c, size_y - 2 + i, tile, :]
+                tile_h[1, 2 * c + i] = fields[3 + c, i, tile, :]
+            tile_h[0, 6 + i] = permit[size_y - 2 + i, tile, :]
+            tile_h[1, 6 + i] = permit[i, tile, :]
+        for c in range(6):
+            value = fields[c, size_y - 3, tile, :]
+            tile_f[0, c] = jnp.where(gz == 0, value, turn(value, 1, 0))[4:]
+            if c < 3:
+                value = fields[c, 2, tile, :]
+                tile_f[1, c] = jnp.where(gz == 0, turn(value, -1, 0), value)[:4]
         eight = iota((8, LANES), 1)
         packed = jnp.full((8, LANES), COURANT, F32)
         for c in range(7):
@@ -464,14 +487,14 @@
 
     start_regions((1,))
     start_regions((3,))
+    for copy in loading[1:3] + loading[4:]:
+        copy.wait()
     for _ in stage(0, *(fields[c] for c in range(3)), (fields[3], fields[5]), (fields[3], fields[4]), (fields[4], fields[5])):
         pass
     start_halo(0, (4, 5, 8, 11, 9, 10, 0, 1, 2, 3, 6, 7))
     fill_regions()
     for n in range(STEPS):
         fill_halo(n)
-    for copy in loading[1:3]:
-        copy.wait()
     geometry()
     run_s, run_c = sincos((phase[0] + 0.5 * ANGULAR_STEP * (iota((8, LANES), 0).astype(F32) + 1.0)) * (0.5 / math.pi))
     for n in range(STEPS):
@@ -483,8 +506,6 @@
         return carry
 
     lax.fori_loop(0, slabs - 3, relay, 0)
-    for copy in loading[4:]:
-        copy.wait()
 
     def half_of(n):
         return run_c[2 * n : 2 * n + 1, :], run_s[2 * n : 2 * n + 1, :]
@@ -558,8 +579,7 @@
     folded = [
         [
             jnp.concatenate([
-                land_w[dy, part, pl.ds(8, size_z), :],
-                jnp.where(iota((8, LANES), 0) < 4, land_w[dy, part, pl.ds(size_z + 8, 8), :], land_w[dy, part, pl.ds(0, 8), :]),
+                land_w[dy, part], land_z[dy, 0, part], land_z[dy, 1, part],
             ], axis=0)
             for part in range(2)
         ]
@@ -590,13 +610,24 @@
         left, right = jnp.where(xy == 0, 1.0, 0.0), jnp.where(xy == 0, 0.0, 1.0)
         behind, ahead = jnp.where(dev > 0, COURANT, 0.0), jnp.where(dev < devs - 1, COURANT, 0.0)
 
-        def rate_of(eps):
-            there = eps > 0.0
-            return jnp.where(there, COURANT / jnp.where(there, eps, 1.0), 0.0)
-
-        e = [[cap_e[0, c, i] for i in range(3)] + [fields[c, y, tile, :] for y in range(size_y)] + [cap_e[1, c, i] for i in range(3)] for c in range(3)]
-        h = [[cap_h[0, c, i] for i in range(3)] + [fields[3 + c, y, tile, :] for y in range(size_y)] + [cap_h[1, c, i] for i in range(2)] for c in range(3)]
-        rates = [None] + [rate_of(cap_r[0, i]) for i in range(2)] + [permit[y, tile, :] for y in range(size_y)] + [rate_of(cap_r[1, i]) for i in range(2)]
+        missing = jnp.zeros((4, LANES), F32)
+
+        def behind_far(half):
+            value = jnp.concatenate([missing, half], axis=0)
+            return jnp.where(gz == 0, value, turn(value, -1, 0))
+
+        def ahead_far(half):
+            value = jnp.concatenate([half, missing], axis=0)
+            return jnp.where(gz == 0, turn(value, 1, 0), value)
+
+        def column(c, held_far, near, offset, ahead_too):
+            planes = [behind_far(held_far)] + [near[0, 2 * offset + i] for i in range(2)]
+            planes += [fields[c, y, tile, :] for y in range(size_y)] + [near[1, 2 * offset + i] for i in range(2)]
+            return planes + ([ahead_far(cap_f[1, offset])] if ahead_too else [])
+
+        e = [column(c, cap_f[0, c], cap_e, c, True) for c in range(3)]
+        h = [column(3 + c, cap_f[0, 3 + c], cap_h, c, False) for c in range(3)]
+        rates = [None] + [cap_h[0, 6 + i] for i in range(2)] + [permit[y, tile, :] for y in range(size_y)] + [cap_h[1, 6 + i] for i in range(2)]
         coefs = [behind] * depth + [COURANT] * size_y + [ahead] * depth
 
         def next_x(value, border, i):
@@ -706,7 +737,7 @@
         return pltpu.make_async_remote_copy(
             src_ref=held,
             dst_ref=held,
-            send_sem=wall_send,
+            send_sem=loads.at[8],
             recv_sem=wall_got,
             device_id={"gz": (gz + k) % slabs},
             device_id_type=MESH,
@@ -770,7 +801,7 @@
         return pltpu.make_async_remote_copy(
             src_ref=parts_out.at[pl.ds(owner * per, per)],
             dst_ref=parts_in.at[source],
-            send_sem=part_send,
+            send_sem=loads.at[0],
             recv_sem=part_got,
             device_id=ident(flat_of(owner)),
             device_id_type=MESH,
@@ -813,7 +844,7 @@
         return pltpu.make_async_remote_copy(
             src_ref=held,
             dst_ref=held,
-            send_sem=total_send,
+            send_sem=loads.at[3],
             recv_sem=total_got.at[owner // together],
             device_id=ident((me + k) % peers),
             device_id_type=MESH,
@@ -823,7 +854,7 @@
     def _():
         everyone = parts_in.at[pl.ds(0, peers - 1)]
         pltpu.make_async_remote_copy(
-            src_ref=everyone, dst_ref=everyone, send_sem=part_send, recv_sem=part_got, device_id={"gz": gz}, device_id_type=MESH
+            src_ref=everyone, dst_ref=everyone, send_sem=loads.at[0], recv_sem=part_got, device_id={"gz": gz}, device_id_type=MESH
         ).wait_recv()
         parts_in[me] = parts_out[pl.ds(mine * per, per)]
         totals[pl.ds(mine * per, per)] = jnp.sum(parts_in[...], axis=0)
@@ -944,11 +975,11 @@
         @pl.when(sent)
         def _():
             everything = arrivals.at[pl.ds(0, rows_sent)]
-            pltpu.make_async_copy(everything, everything, halo_send.at[group]).wait()
+            pltpu.make_async_copy(everything, everything, sent_by(group)).wait()
 
     def parts_sent(ref):
         pltpu.make_async_remote_copy(
-            src_ref=ref, dst_ref=ref, send_sem=part_send, recv_sem=part_got, device_id={"gz": gz}, device_id_type=MESH
+            src_ref=ref, dst_ref=ref, send_sem=loads.at[0], recv_sem=part_got, device_id={"gz": gz}, device_id_type=MESH
         ).wait_send()
 
     @pl.when(leads)
@@ -1018,13 +1049,14 @@
             pltpu.VMEM((5, size_y, 1, LANES), F32),
             pltpu.VMEM((376, 1, LANES), F32),
             pltpu.VMEM((2, size_z, LANES), F32),
+            pltpu.VMEM((2, 2, 4, LANES), F32),
             pltpu.VMEM((8, LANES), F32),
-            pltpu.VMEM((3, 2, size_z + 16, LANES), F32),
+            pltpu.VMEM((3, 2, size_z, LANES), F32),
+            pltpu.VMEM((3, 2, 2, 4, LANES), F32),
             pltpu.VMEM((3, 2, 8, LANES), F32),
-            pltpu.VMEM((2, 3, 3, 8, LANES), F32),
-            pltpu.VMEM((2, 3, 3, 8, LANES), F32),
-            pltpu.VMEM((2, 2, 8, LANES), F32),
-            pltpu.VMEM((3, 3, 8, LANES), F32),
+            *(pltpu.VMEM(shape, F32) for shape in ((2, 6, 8, LANES), (2, 8, 8, LANES), (2, 6, 4, LANES)) * 2),
+            pltpu.VMEM((8, 8, LANES), F32),
+            pltpu.VMEM((6, 4, LANES), F32),
             pltpu.VMEM((8 * size_y, LANES), F32),
             pltpu.VMEM(fields.shape, F32),
             pltpu.VMEM(spectra.shape, F32),
@@ -1047,10 +1079,8 @@
             pltpu.VMEM((chunks, 4, LANES), F32),
             pltpu.VMEM((slabs, 8, LANES), F32),
             pltpu.VMEM((2, cap_count, LANES), F32),
-            dma((len(halos) + 5,)), dma((STEPS,)),
-            dma, dma,
-            dma, dma((owners // max(1, 4 // per),)),
-            dma, dma,
+            dma((11,)), dma((STEPS,)),
+            dma, dma((owners // max(1, 4 // per),)), dma,
             dma, dma((2,)),
             dma((9,)), pltpu.SemaphoreType.REGULAR((2,)), dma((3,)),
         ],

time: 21.6 us -> 21.2 us (0.981)
  Pallas kernels: 20.2 us -> 19.8 us
    pallas_call x1, Pallas kernels: 19.3 us -> 18.9 us  [local(): pl.pallas_call(functools.partial(kernel, (slabs, devs, xys)), out_shape=(...]
where the time goes in v7:
time: 21.2 us; the launch traced here: 21 us
  Pallas kernels  19.8 us (93%)
  between operations  1.29 us (6%)
    pallas_call x1, Pallas kernels, local(): pl.pallas_call(functools.partial(kernel, (slabs, devs, xys)), out_shape=(...  18.9 us
    pallas_call x1, Pallas kernels, local(): pl.pallas_call(write_out, out_shape=tuple((jax.ShapeDtypeStruct(shape, F3...  0.86 us

profile of v7, /device:TPU:0, one launch (start us, length us, event | category | flops | bytes accessed | tf_op | source)
XLA Modules:
  0.0 21.0 jit_solution(17410199871636312614)
XLA Ops:
  1.3 18.9 %shard_map.128 = (f32[6,4,16,128]{3,2,1,0:T(8,128)S(1)}, f32[12,4,16,128]{3,2,1,0:T(8,128)S(1)}, f32[20,1,128]{2,1,0:T(1,128)S(1)}, f32[1,128]{1,0:T(1,128)S(1)}, f32[36,1,128]{2,1,0:T(1,128)S(1)}) custom-call(f32[6,4,16,128]{3,2,1,0:T(8,128)} %fields_in.1, f32[12,4,16,128]{3,2,1,0:T(8,128)} %spectra_in.1, f32[4,16,128]{2,1,0:T(8,128)} %permit_in.1, ...), custom_call_target="tpu_custom_call" | custom-call | tf_op jit(solution)/shard_map/pallas_call | solution.py:1034
  20.2 0.9 %shard_map.129 = (f32[6,4,16,128]{3,2,1,0:T(8,128)}, f32[12,4,16,128]{3,2,1,0:T(8,128)}, f32[20,1,128]{2,1,0:T(1,128)}, f32[1,128]{1,0:T(1,128)}, f32[36,1,128]{2,1,0:T(1,128)}) custom-call(f32[6,4,16,128]{3,2,1,0:T(8,128)S(1)} %get-tuple-element.15.refs_0_, f32[12,4,16,128]{3,2,1,0:T(8,128)S(1)} %get-tuple-element.16.refs_1_, ...), custom_call_target="tpu_custom_call" | custom-call | tf_op jit(solution)/shard_map/pallas_call | solution.py:1093

commit v8 on v7

--- a/solution.py
+++ b/solution.py
@@ -75,7 +75,7 @@
     fields, spectra, permit, phase, wall_owner, cap_owner, dirs, target, aim,
     geo, weights, phases, table_hi, table_lo, cap_plane, lhs,
     parts_out, parts_in, totals, walls, caps,
-    halo_send, halo_got, part_got, total_got, wall_got, cap_send, cap_got, loads, chain, region_got,
+    halo_send, halo_got, part_got, total_got, wall_got, loads, chain, region_got,
 ):
     slabs, devs, xys = sizes
     peers = slabs * devs * xys
@@ -359,9 +359,9 @@
     for at, a in enumerate((1, -1)):
         far_count = 6 if a > 0 else 3
         for kind, source, landing, nothing in (
-            (2, tile_e.at[at], cap_e.at[at], empty.at[pl.ds(0, 6)]),
+            (3, tile_e.at[at], cap_e.at[at], empty.at[pl.ds(0, 6)]),
             (3, tile_h.at[at], cap_h.at[at], empty),
-            (3, tile_f.at[at, pl.ds(0, far_count)], cap_f.at[at, pl.ds(0, far_count)], empty_half.at[pl.ds(0, far_count)]),
+            (2, tile_f.at[at, pl.ds(0, far_count)], cap_f.at[at, pl.ds(0, far_count)], empty_half.at[pl.ds(0, far_count)]),
         ):
             regions.append((kind, {"dev": a}, source, landing, landing, nothing))
 
@@ -386,7 +386,7 @@
             src_ref=source,
             dst_ref=landing,
             send_sem=sent_by(group_of(number)),
-            recv_sem=region_got.at[min(kind, 2)],
+            recv_sem=region_got.at[0 if kind < 2 else 1],
             device_id=to,
             device_id_type=MESH,
         )
@@ -408,12 +408,12 @@
 
             @pl.when(jnp.logical_and(missing, is_end) if kind else missing)
             def _():
-                pltpu.make_async_copy(nothing, landing, region_got.at[min(kind, 2)]).start()
+                pltpu.make_async_copy(nothing, landing, region_got.at[0 if kind < 2 else 1]).start()
 
     def wait_region(which):
-        length = (4 * size_z + 6 * 8, 5 * 8, 2 * (6 + 8) * 8 + (6 + 3) * 4)[which]
+        length = (4 * size_z + 6 * 8, 4 * size_z + 6 * 8 + 5 * 8, 2 * (6 + 8) * 8 + (6 + 3) * 4)[which]
         everything = arrivals.at[pl.ds(0, length)]
-        pltpu.make_async_copy(everything, everything, region_got.at[which]).wait()
+        pltpu.make_async_copy(everything, everything, region_got.at[which // 2]).wait()
 
     def window(slots, amount_of):
         rows = slots[0].shape[1]
@@ -439,10 +439,12 @@
     @pl.when(is_end)
     def _():
         tile = pl.ds(zt, 8)
-        for c in range(3):
-            for i in range(2):
-                tile_e[0, 2 * c + i] = fields[c, size_y - 2 + i, tile, :]
-                tile_e[1, 2 * c + i] = fields[c, i, tile, :]
+        for c in range(6):
+            value = fields[c, size_y - 3, tile, :]
+            tile_f[0, c] = jnp.where(gz == 0, value, turn(value, 1, 0))[4:]
+            if c < 3:
+                value = fields[c, 2, tile, :]
+                tile_f[1, c] = jnp.where(gz == 0, turn(value, -1, 0), value)[:4]
 
     start_regions((2,))
     loading[3].wait()
@@ -464,12 +466,10 @@
                 tile_h[1, 2 * c + i] = fields[3 + c, i, tile, :]
             tile_h[0, 6 + i] = permit[size_y - 2 + i, tile, :]
             tile_h[1, 6 + i] = permit[i, tile, :]
-        for c in range(6):
-            value = fields[c, size_y - 3, tile, :]
-            tile_f[0, c] = jnp.where(gz == 0, value, turn(value, 1, 0))[4:]
-            if c < 3:
-                value = fields[c, 2, tile, :]
-                tile_f[1, c] = jnp.where(gz == 0, turn(value, -1, 0), value)[:4]
+        for c in range(3):
+            for i in range(2):
+                tile_e[0, 2 * c + i] = fields[c, size_y - 2 + i, tile, :]
+                tile_e[1, 2 * c + i] = fields[c, i, tile, :]
         eight = iota((8, LANES), 1)
         packed = jnp.full((8, LANES), COURANT, F32)
         for c in range(7):
@@ -562,11 +562,13 @@
             ez = ez + r * ((hy - turn(hy, 1, 1)) - (hx - turn(hx, 8, 1)))
             visit(n, before, ey, ez, hy, hz)
 
-    wait_region(0)
-
     @pl.when(is_end)
     def _():
         wait_region(1)
+
+    @pl.when(jnp.logical_not(is_end))
+    def _():
+        wait_region(0)
 
     sums = [jnp.zeros((size_z, LANES), F32) for _ in range(8)]
 
@@ -747,16 +749,18 @@
         return pltpu.make_async_remote_copy(
             src_ref=caps.at[at],
             dst_ref=caps.at[at],
-            send_sem=cap_send,
-            recv_sem=cap_got.at[at],
+            send_sem=loads.at[8],
+            recv_sem=wall_got,
             device_id={"gz": (gz + k) % slabs},
             device_id_type=MESH,
         )
 
     sign = jnp.where(sub < 4, -1.0, 1.0)
 
+    far_rows = lhs[...]
+
     def far_of(j):
-        rows = lhs[...]
+        rows = far_rows
         by_high = jnp.dot(rows, table_hi[j], preferred_element_type=F32)
         by_low = jnp.dot(rows[:all_rows], table_lo[j], preferred_element_type=F32)
         product = by_high[:all_rows] + by_high[all_rows:] + by_low
@@ -823,7 +827,11 @@
         return carry
 
     hear()
-    lax.fori_loop(0, owners // together, far_and_send, 0)
+    lax.fori_loop(0, owners // together, far_and_send, 0, unroll=True)
+
+    @pl.when(leads)
+    def _():
+        parts_in[me] = parts_out[pl.ds(mine * per, per)]
 
     ghosts = advance(0, None)
     for y in range(size_y):
@@ -856,7 +864,6 @@
         pltpu.make_async_remote_copy(
             src_ref=everyone, dst_ref=everyone, send_sem=loads.at[0], recv_sem=part_got, device_id={"gz": gz}, device_id_type=MESH
         ).wait_recv()
-        parts_in[me] = parts_out[pl.ds(mine * per, per)]
         totals[pl.ds(mine * per, per)] = jnp.sum(parts_in[...], axis=0)
         for k in sorted(range(slabs), key=lambda k: -min(k, slabs - k)):
             row = (gz + k) % slabs * across
@@ -883,11 +890,12 @@
         return jnp.dot(chooser, records, precision=HIGHEST, preferred_element_type=F32)[:share]
 
     def choose_owned():
-        wall_copy(1, walls.at[pl.ds(0, slabs - 1)]).wait_recv()
-        for at, holder in enumerate((0, slabs - 1)):
-            @pl.when(gz != holder)
+        for ends, caps_due in ((is_end, 1), (jnp.logical_not(is_end), 2)):
+            @pl.when(ends)
             def _():
-                cap_copy(1, at).wait_recv()
+                everything = arrivals.at[pl.ds(0, 8 * (slabs - 1) + caps_due * caps.shape[1])]
+                pltpu.make_async_copy(everything, everything, wall_got).wait()
+
         all_walls = walls[...]
         owner_all = jnp.sum(all_walls[:, size_y : size_y + 1, :], axis=0)[:, : 8 * slabs]
         cap_share = (owned_out.shape[0] - size_y) // 2
@@ -991,12 +999,11 @@
     def _():
         parts_sent(parts_out)
 
-    wall_copy(1, walls.at[pl.ds(0, slabs - 1)]).wait_send()
-    for at, holder in enumerate((0, slabs - 1)):
-        @pl.when(gz == holder)
+    for ends, caps_sent in ((is_end, 1), (jnp.logical_not(is_end), 0)):
+        @pl.when(ends)
         def _():
-            sent = weights.at[pl.ds(0, slabs - 1)]
-            pltpu.make_async_copy(sent, sent, cap_send).wait()
+            everything = arrivals.at[pl.ds(0, (slabs - 1) * (8 + caps_sent * caps.shape[1]))]
+            pltpu.make_async_copy(everything, everything, loads.at[8]).wait()
 
 
 def write_out(*refs):
@@ -1047,7 +1054,7 @@
             *(pltpu.VMEM(shape, F32) for shape in halos),
             pltpu.VMEM((5, size_z, LANES), F32),
             pltpu.VMEM((5, size_y, 1, LANES), F32),
-            pltpu.VMEM((376, 1, LANES), F32),
+            pltpu.VMEM((max(376, (slabs - 1) * (8 + cap_count)), 1, LANES), F32),
             pltpu.VMEM((2, size_z, LANES), F32),
             pltpu.VMEM((2, 2, 4, LANES), F32),
             pltpu.VMEM((8, LANES), F32),
@@ -1081,8 +1088,7 @@
             pltpu.VMEM((2, cap_count, LANES), F32),
             dma((11,)), dma((STEPS,)),
             dma, dma((owners // max(1, 4 // per),)), dma,
-            dma, dma((2,)),
-            dma((9,)), pltpu.SemaphoreType.REGULAR((2,)), dma((3,)),
+            dma((9,)), pltpu.SemaphoreType.REGULAR((2,)), dma((2,)),
         ],
         compiler_params=pltpu.CompilerParams(collective_id=0, has_side_effects=True),
     )(

time: 21.2 us -> 21.2 us (level)
  no operation moved by 1% of the time
where the time goes in v8:
time: 21.2 us; the launch traced here: 21 us
  Pallas kernels  19.7 us (93%)
  between operations  1.29 us (6%)
    pallas_call x1, Pallas kernels, local(): pl.pallas_call(functools.partial(kernel, (slabs, devs, xys)), out_shape=(...  18.9 us
    pallas_call x1, Pallas kernels, local(): pl.pallas_call(write_out, out_shape=tuple((jax.ShapeDtypeStruct(shape, F3...  0.86 us

profile of v8, /device:TPU:0, one launch (start us, length us, event | category | flops | bytes accessed | tf_op | source)
XLA Modules:
  0.0 21.0 jit_solution(10388444052895410769)
XLA Ops:
  1.3 18.9 %shard_map.128 = (f32[6,4,16,128]{3,2,1,0:T(8,128)S(1)}, f32[12,4,16,128]{3,2,1,0:T(8,128)S(1)}, f32[20,1,128]{2,1,0:T(1,128)S(1)}, f32[1,128]{1,0:T(1,128)S(1)}, f32[36,1,128]{2,1,0:T(1,128)S(1)}) custom-call(f32[6,4,16,128]{3,2,1,0:T(8,128)} %fields_in.1, f32[12,4,16,128]{3,2,1,0:T(8,128)} %spectra_in.1, f32[4,16,128]{2,1,0:T(8,128)} %permit_in.1, ...), custom_call_target="tpu_custom_call" | custom-call | tf_op jit(solution)/shard_map/pallas_call | solution.py:1041
  20.2 0.9 %shard_map.129 = (f32[6,4,16,128]{3,2,1,0:T(8,128)}, f32[12,4,16,128]{3,2,1,0:T(8,128)}, f32[20,1,128]{2,1,0:T(1,128)}, f32[1,128]{1,0:T(1,128)}, f32[36,1,128]{2,1,0:T(1,128)}) custom-call(f32[6,4,16,128]{3,2,1,0:T(8,128)S(1)} %get-tuple-element.15.refs_0_, f32[12,4,16,128]{3,2,1,0:T(8,128)S(1)} %get-tuple-element.16.refs_1_, ...), custom_call_target="tpu_custom_call" | custom-call | tf_op jit(solution)/shard_map/pallas_call | solution.py:1099

commit v9 on v8

--- a/solution.py
+++ b/solution.py
@@ -489,9 +489,6 @@
     start_regions((3,))
     for copy in loading[1:3] + loading[4:]:
         copy.wait()
-    for _ in stage(0, *(fields[c] for c in range(3)), (fields[3], fields[5]), (fields[3], fields[4]), (fields[4], fields[5])):
-        pass
-    start_halo(0, (4, 5, 8, 11, 9, 10, 0, 1, 2, 3, 6, 7))
     fill_regions()
     for n in range(STEPS):
         fill_halo(n)
@@ -499,6 +496,10 @@
     run_s, run_c = sincos((phase[0] + 0.5 * ANGULAR_STEP * (iota((8, LANES), 0).astype(F32) + 1.0)) * (0.5 / math.pi))
     for n in range(STEPS):
         tables_of(n)
+
+    for _ in stage(0, *(fields[c] for c in range(3)), (fields[3], fields[5]), (fields[3], fields[4]), (fields[4], fields[5])):
+        pass
+    start_halo(0, (4, 5, 8, 11, 9, 10, 0, 1, 2, 3, 6, 7))
 
     def relay(k, carry):
         hear()

time: 21.2 us -> 20.8 us (0.981)
  Pallas kernels: 19.7 us -> 19.4 us
    pallas_call x1, Pallas kernels: 18.9 us -> 18.5 us  [local(): pl.pallas_call(functools.partial(kernel, (slabs, devs, xys)), out_shape=(...]
where the time goes in v9:
time: 20.8 us; the launch traced here: 20.6 us
  Pallas kernels  19.4 us (93%)
  between operations  1.29 us (6%)
    pallas_call x1, Pallas kernels, local(): pl.pallas_call(functools.partial(kernel, (slabs, devs, xys)), out_shape=(...  18.5 us
    pallas_call x1, Pallas kernels, local(): pl.pallas_call(write_out, out_shape=tuple((jax.ShapeDtypeStruct(shape, F3...  0.86 us

profile of v9, /device:TPU:0, one launch (start us, length us, event | category | flops | bytes accessed | tf_op | source)
XLA Modules:
  0.0 20.6 jit_solution(9336189532934315681)
XLA Ops:
  1.3 18.5 %shard_map.128 = (f32[6,4,16,128]{3,2,1,0:T(8,128)S(1)}, f32[12,4,16,128]{3,2,1,0:T(8,128)S(1)}, f32[20,1,128]{2,1,0:T(1,128)S(1)}, f32[1,128]{1,0:T(1,128)S(1)}, f32[36,1,128]{2,1,0:T(1,128)S(1)}) custom-call(f32[6,4,16,128]{3,2,1,0:T(8,128)} %fields_in.1, f32[12,4,16,128]{3,2,1,0:T(8,128)} %spectra_in.1, f32[4,16,128]{2,1,0:T(8,128)} %permit_in.1, ...), custom_call_target="tpu_custom_call" | custom-call | tf_op jit(solution)/shard_map/pallas_call | solution.py:1042
  19.8 0.9 %shard_map.129 = (f32[6,4,16,128]{3,2,1,0:T(8,128)}, f32[12,4,16,128]{3,2,1,0:T(8,128)}, f32[20,1,128]{2,1,0:T(1,128)}, f32[1,128]{1,0:T(1,128)}, f32[36,1,128]{2,1,0:T(1,128)}) custom-call(f32[6,4,16,128]{3,2,1,0:T(8,128)S(1)} %get-tuple-element.15.refs_0_, f32[12,4,16,128]{3,2,1,0:T(8,128)S(1)} %get-tuple-element.16.refs_1_, ...), custom_call_target="tpu_custom_call" | custom-call | tf_op jit(solution)/shard_map/pallas_call | solution.py:1100
